TPU v7x, 32 devices: a whole 2x2x4 slice. The times are simulated.
32 devices in a mesh: rows: 8 (over z, y), wide: 4 (over x, core).
Axes of the slice: x: 2, y: 2, z: 4, core: 2. Of those that a mesh axis runs over, the one named last changes fastest.
Arguments:
- tokens: bfloat16 [16, 1024, 1024], P('rows', 'wide'), may hold values from -6 to 6
- doc_ids: int32 [16, 1024], P('rows'), may hold values from 0 to 5, never falling along the last dimension, each value on 1 to 512 neighbouring positions
- factor_weight: bfloat16 [1024, 800], replicated, may hold values from -0.3125 to 0.3125
- output_weight: bfloat16 [1024, 1024], replicated, may hold values from -0.5 to 0.5
- norm_one: float32 [1024], replicated, may hold values from 0.5 to 1.5
- norm_two: float32 [1024], replicated, may hold values from 0.5 to 1.5
- gate_weight: bfloat16 [1024, 2816], P(None, 'wide'), may hold values from -0.1875 to 0.1875
- up_weight: bfloat16 [1024, 2816], P(None, 'wide'), may hold values from -0.1875 to 0.1875
- down_weight: bfloat16 [2816, 1024], P('wide'), may hold values from -0.15625 to 0.15625
- cotangent: bfloat16 [16, 1024, 1024], P('rows', 'wide'), may hold values from -6 to 6
Outputs:
- output: bfloat16 [16, 1024, 1024], P('rows', 'wide')
- input_grad: bfloat16 [16, 1024, 1024], P('rows', 'wide')
- grad_factors: float32 [1024, 800], replicated
- grad_out: float32 [1024, 1024], replicated
- grad_norm_one: float32 [1024], replicated
- grad_norm_two: float32 [1024], replicated
- grad_gate: float32 [1024, 2816], P(None, 'wide')
- up_weight_gradient: float32 [1024, 2816], P(None, 'wide')
- down_weight_gradient: float32 [2816, 1024], P('wide')
Inputs may be any that keep to these rules, and one draw needn't show every extreme that they name: `doc_ids`: in each sequence the ids never fall along the positions; a document holds 1 to 512 positions, and one document of every sequence holds exactly 512.
All inputs are finite; a program needn't handle non-finite values.
Results may differ from a plain program's by a relative error of at most 0.017.
The roundings to bfloat16 on the way count: a program that leaves them out, or rounds other values in their place, can miss the bound.
Values may be sent and summed in bfloat16 or wider, within the bound.
A program may use at most 256 MiB of HBM per device.

v0:
```python
import functools

import jax
import jax.numpy as jnp
from jax import lax
from jax.experimental import pallas as pl
from jax.experimental.pallas import tpu as pltpu
from jax.sharding import PartitionSpec as P

H = 16
DH = 64
RQ = 6
RK = 2
MAX_DOC = 512
EPS = 1e-06
NEG = -1000000000.0
BIG = 3.0e38

QA = H * RQ
QCOLS = QA + RQ * DH
KA = H * RK
KCOLS = KA + RK * DH
KV = 2 * KCOLS
QPAD = 512
KPAD = 384
PAIRS = H // 2

F32 = jnp.float32
BF16 = jnp.bfloat16

NN = (((1,), (0,)), ((), ()))
NT = (((1,), (1,)), ((), ()))
TN = (((0,), (0,)), ((), ()))


def mm(a, b, dims=NN):
    return lax.dot_general(a, b, dims, preferred_element_type=F32)


def params(vmem_mb=60):
    return pltpu.CompilerParams(vmem_limit_bytes=vmem_mb << 20)


def cost(flops, nbytes):
    return pl.CostEstimate(flops=int(flops), bytes_accessed=int(nbytes), transcendentals=0)


def selection(shape, rule):
    row = lax.broadcasted_iota(jnp.int32, shape, 0)
    col = lax.broadcasted_iota(jnp.int32, shape, 1)
    return jnp.where(rule(row, col), 1.0, 0.0).astype(BF16)


def head_spread(pair, base, rank, shape):
    def rule(row, col):
        r = col // 128
        lane = col - r * 128
        head = 2 * pair + jnp.where(lane >= DH, 1, 0)
        return row == base + head * rank + r

    return selection(shape, rule)


def rank_tile(base, shape):
    def rule(row, col):
        r = col // 128
        lane = col - r * 128
        return row == base + r * DH + jnp.where(lane >= DH, lane - DH, lane)

    return selection(shape, rule)


def front_kernel(x_ref, w_ref, g_ref, n_ref, q_ref, kv_ref):
    x = x_ref[...].astype(F32)
    r = lax.rsqrt(jnp.mean(x * x, axis=-1, keepdims=True) + EPS)
    n = (x * r * g_ref[...]).astype(BF16)
    n_ref[...] = n
    f = mm(n, w_ref[...]).astype(BF16)
    q_ref[...] = f[:, :QPAD]
    kv_ref[:, :KV] = f[:, QCOLS:]
    kv_ref[:, KV:] = jnp.zeros((f.shape[0], KPAD - KV), BF16)


def front(x, w, gain):
    rows, d = x.shape
    blk = 256 if rows % 256 == 0 else rows
    return pl.pallas_call(
        front_kernel,
        grid=(rows // blk,),
        in_specs=[
            pl.BlockSpec((blk, d), lambda i: (i, 0)),
            pl.BlockSpec(w.shape, lambda i: (0, 0)),
            pl.BlockSpec((1, d), lambda i: (0, 0)),
        ],
        out_specs=[
            pl.BlockSpec((blk, d), lambda i: (i, 0)),
            pl.BlockSpec((blk, QPAD), lambda i: (i, 0)),
            pl.BlockSpec((blk, KPAD), lambda i: (i, 0)),
        ],
        out_shape=[
            jax.ShapeDtypeStruct((rows, d), BF16),
            jax.ShapeDtypeStruct((rows, QPAD), BF16),
            jax.ShapeDtypeStruct((rows, KPAD), BF16),
        ],
        compiler_params=params(),
        cost_estimate=cost(2 * rows * d * 800, rows * d * 6 + d * 1600),
        name="front",
    )(x, w, gain)


def make_cap(s_ref, dq_ref, dk_ref, cap_ref, nblk, own):
    dq = dq_ref[...]
    for i in range(nblk):
        rows = pl.ds(i * own, own)
        key = lax.broadcasted_iota(jnp.int32, (own, own), 0)
        query = lax.broadcasted_iota(jnp.int32, (own, own), 1) + s_ref[1 + i]
        ok = (dk_ref[rows, :] == dq) & (key <= query)
        cap_ref[rows, :] = jnp.where(ok, BIG, NEG)


def stacked(x):
    lane = lax.broadcasted_iota(jnp.int32, x.shape, 1)
    zero = jnp.zeros_like(x)
    return jnp.concatenate(
        [jnp.where(lane < DH, x, zero), jnp.where(lane >= DH, x, zero)], axis=0
    )


def unstacked(xt, own):
    pair = jnp.concatenate([xt[:DH, :own], xt[DH:, own:]], axis=0)
    return pair.T


def key_parts(kvf_ref, pair):
    ek = head_spread(pair, 0, RK, (128, RK * 128))
    ev = head_spread(pair, KCOLS - 128, RK, (128, RK * 128))
    ke = mm(kvf_ref[:, :128], ek)
    ve = mm(kvf_ref[:, 128:256], ev)
    return ke, ve


def tile_keys(kvf_ref, bk_ref, bv_ref):
    bk_ref[...] = mm(kvf_ref[:, :256], rank_tile(KA, (256, RK * 128)))
    bv_ref[...] = mm(kvf_ref[:, 128:384], rank_tile(KCOLS + KA - 128, (256, RK * 128)))


def attend_kernel(
    nblk, s_ref, qf_ref, kvg_ref, dq_ref, dk_ref, x_ref, wo_ref, g_ref,
    att_ref, q_ref, k_ref, v_ref, lse_ref, hm_ref, n_ref, kvw_ref,
    bq_ref, bk_ref, bv_ref, cap_ref, full_ref,
):
    pair = pl.program_id(0)
    own = qf_ref.shape[0]

    @pl.when(pair == 0)
    def _():
        for i in range(nblk):
            kvw_ref[pl.ds(i * own, own), :] = kvg_ref[s_ref[1 + nblk + i]]
        bq_ref[...] = mm(qf_ref[...], rank_tile(QA, (QPAD, RQ * 128)))
        tile_keys(kvw_ref, bk_ref, bv_ref)
        make_cap(s_ref, dq_ref, dk_ref, cap_ref, nblk, own)

    qe = mm(qf_ref[:, :128], head_spread(pair, 0, RQ, (128, RQ * 128)))
    qsum = qe[:, :128] * bq_ref[:, :128]
    for r in range(1, RQ):
        cols = slice(r * 128, (r + 1) * 128)
        qsum = qsum + qe[:, cols] * bq_ref[:, cols]
    q = (qsum * (1.0 / RQ)).astype(BF16)
    ke, ve = key_parts(kvw_ref, pair)
    k = ((ke[:, :128] * bk_ref[:, :128] + ke[:, 128:] * bk_ref[:, 128:]) * (1.0 / RK)).astype(BF16)
    v = ((ve[:, :128] * bv_ref[:, :128] + ve[:, 128:] * bv_ref[:, 128:]) * (1.0 / RK)).astype(BF16)
    q = q * jnp.asarray(DH ** (-0.5), BF16)
    q_ref[...] = q
    k_ref[...] = k
    v_ref[...] = v
    cap = cap_ref[...]
    st = jnp.minimum(mm(k, stacked(q), NT), jnp.concatenate([cap, cap], axis=1))
    top = jnp.max(st, axis=0, keepdims=True)
    e = jnp.exp(st - top)
    total = jnp.sum(e, axis=0, keepdims=True)
    p = (e * (1.0 / total)).astype(BF16)
    lse_ref[0] = top + jnp.log(total)
    att = unstacked(mm(v, p, TN), own).astype(BF16)
    att_ref[...] = att
    full_ref[pair] = att

    @pl.when(pair == pl.num_programs(0) - 1)
    def _():
        hm = x_ref[...].astype(F32)
        att_all = jnp.concatenate([full_ref[i] for i in range(PAIRS)], axis=1)
        hm = hm + mm(att_all, wo_ref[...])
        hm_ref[...] = hm
        r = lax.rsqrt(jnp.mean(hm * hm, axis=-1, keepdims=True) + EPS)
        n_ref[...] = (hm * r * g_ref[...]).astype(BF16)


def attend(nblk, scalars, qf, kvg, dq, dk, x, wo, gain):
    own, d = x.shape
    win = nblk * own
    whole = lambda a: pl.BlockSpec(a.shape, lambda p, a=a: (0,) * a.ndim)
    col = lambda rows: pl.BlockSpec((rows, 128), lambda p: (0, p))
    return pl.pallas_call(
        functools.partial(attend_kernel, nblk),
        grid=(PAIRS,),
        in_specs=[pl.BlockSpec(memory_space=pltpu.SMEM)]
        + [whole(a) for a in (qf, kvg, dq, dk, x, wo, gain)],
        out_specs=[
            col(own), col(own), col(win), col(win),
            pl.BlockSpec((1, 1, 2 * own), lambda p: (p, 0, 0)),
            pl.BlockSpec((own, d), lambda p: (0, 0)),
            pl.BlockSpec((own, d), lambda p: (0, 0)),
            pl.BlockSpec((win, KPAD), lambda p: (0, 0)),
        ],
        out_shape=[
            jax.ShapeDtypeStruct((own, d), BF16),
            jax.ShapeDtypeStruct((own, d), BF16),
            jax.ShapeDtypeStruct((win, d), BF16),
            jax.ShapeDtypeStruct((win, d), BF16),
            jax.ShapeDtypeStruct((PAIRS, 1, 2 * own), F32),
            jax.ShapeDtypeStruct((own, d), F32),
            jax.ShapeDtypeStruct((own, d), BF16),
            jax.ShapeDtypeStruct((win, KPAD), BF16),
        ],
        scratch_shapes=[
            pltpu.VMEM((own, RQ * 128), F32),
            pltpu.VMEM((win, RK * 128), F32),
            pltpu.VMEM((win, RK * 128), F32),
            pltpu.VMEM((win, own), F32),
            pltpu.VMEM((PAIRS, own, 128), BF16),
        ],
        compiler_params=params(),
        cost_estimate=cost(12e9, 12e6),
        name="attend",
    )(scalars, qf, kvg, dq, dk, x, wo, gain)


def ffn_kernel(has_prev, bf16_out, *refs):
    if has_prev:
        n_ref, c_ref, wg_ref, wu_ref, wd_ref, pg_ref, pu_ref, pd_ref = refs[:8]
        refs = refs[8:]
    else:
        n_ref, c_ref, wg_ref, wu_ref, wd_ref = refs[:5]
        refs = refs[5:]
    o_ref, dn_ref, og_ref, ou_ref, od_ref = refs[:5]
    if bf16_out:
        ag_ref, au_ref, ad_ref = refs[5:]
    else:
        ag_ref, au_ref, ad_ref = og_ref, ou_ref, od_ref
    step = pl.program_id(0)

    @pl.when(step == 0)
    def _():
        if has_prev:
            ag_ref[...] = pg_ref[...]
            au_ref[...] = pu_ref[...]
            ad_ref[...] = pd_ref[...]
        else:
            ag_ref[...] = jnp.zeros_like(ag_ref)
            au_ref[...] = jnp.zeros_like(au_ref)
            ad_ref[...] = jnp.zeros_like(ad_ref)

    n = n_ref[0]
    c = c_ref[0]
    wg, wu, wd = wg_ref[...], wu_ref[...], wd_ref[...]
    g = mm(n, wg)
    u = mm(n, wu)
    dh = mm(c, wd, NT)
    s = 1.0 / (1.0 + jnp.exp(-g))
    gs = g * s
    hid = (gs * u).astype(BF16)
    dg = (dh * u * (s * (1.0 + g * (1.0 - s)))).astype(BF16)
    du = (dh * gs).astype(BF16)
    o_ref[0] = mm(hid, wd).astype(BF16)
    dn_ref[0] = (mm(dg, wg, NT) + mm(du, wu, NT)).astype(BF16)
    ag_ref[...] += mm(n, dg, TN)
    au_ref[...] += mm(n, du, TN)
    ad_ref[...] += mm(hid, c, TN)
    if bf16_out:

        @pl.when(step == pl.num_programs(0) - 1)
        def _():
            og_ref[...] = ag_ref[...].astype(BF16)
            ou_ref[...] = au_ref[...].astype(BF16)
            od_ref[...] = ad_ref[...].astype(BF16)


def ffn(n, c, wg, wu, wd, prev, last):
    w, own, d = n.shape
    ff = wg.shape[1]
    one = lambda a: pl.BlockSpec(
        a.shape, lambda i, a=a: (0,) * a.ndim, pipeline_mode=pl.Buffered(1)
    )
    blk = pl.BlockSpec((1, own, d), lambda i: (i, 0, 0))
    dt = BF16 if last else F32
    args = [n, c, wg, wu, wd] + list(prev or [])
    shapes = [(d, ff), (d, ff), (ff, d)]
    return pl.pallas_call(
        functools.partial(ffn_kernel, bool(prev), last),
        grid=(w,),
        in_specs=[blk, blk] + [one(a) for a in args[2:]],
        out_specs=[blk, blk] + [
            pl.BlockSpec(s, lambda i: (0, 0), pipeline_mode=pl.Buffered(1)) for s in shapes
        ],
        out_shape=[jax.ShapeDtypeStruct(n.shape, BF16)] * 2
        + [jax.ShapeDtypeStruct(s, dt) for s in shapes],
        scratch_shapes=[pltpu.VMEM(s, F32) for s in shapes] if last else [],
        compiler_params=params(),
        cost_estimate=cost(18 * w * own * d * ff, 20 * w * own * d),
        name="ffn",
    )(*args)


def back_kernel(
    nblk, s_ref, q_ref, k_ref, v_ref, lse_ref, dq_ref, dk_ref, qf_ref, kvw_ref,
    dn_ref, hm_ref, c_ref, wo_ref, g_ref,
    dm_ref, dl_ref, gain_ref, gq_ref, gkv_ref,
    bq_ref, bk_ref, bv_ref, cap_ref, da_ref, aq_ref, ak_ref, av_ref, tq_ref, tk_ref, tv_ref,
):
    pair = pl.program_id(0)
    own = q_ref.shape[0]
    last = pl.num_programs(0) - 1

    @pl.when(pair == 0)
    def _():
        hm = hm_ref[...]
        dn = dn_ref[...].astype(F32)
        r = lax.rsqrt(jnp.mean(hm * hm, axis=-1, keepdims=True) + EPS)
        z = dn * g_ref[...]
        gain_ref[...] = jnp.sum(dn * hm * r, axis=0, keepdims=True)
        dm = (
            c_ref[...].astype(F32)
            + r * z
            - hm * (r * r * r) * jnp.mean(z * hm, axis=-1, keepdims=True)
        )
        dm_ref[...] = dm
        low = dm.astype(BF16)
        dl_ref[...] = low
        da = mm(low, wo_ref[...], NT).astype(BF16)
        for i in range(PAIRS):
            da_ref[i] = da[:, i * 128:(i + 1) * 128]
        bq_ref[...] = mm(qf_ref[...], rank_tile(QA, (QPAD, RQ * 128)))
        tile_keys(kvw_ref, bk_ref, bv_ref)
        make_cap(s_ref, dq_ref, dk_ref, cap_ref, nblk, own)
        for ref in (aq_ref, ak_ref, av_ref, tq_ref, tk_ref, tv_ref):
            ref[...] = jnp.zeros_like(ref)

    q = q_ref[...]
    k = k_ref[...]
    v = v_ref[...]
    qs = stacked(q)
    ds_ = stacked(da_ref[pair])
    cap = cap_ref[...]
    st = jnp.minimum(mm(k, qs, NT), jnp.concatenate([cap, cap], axis=1))
    p = jnp.exp(st - lse_ref[0])
    dp = mm(v, ds_, NT)
    delta = jnp.sum(p * dp, axis=0, keepdims=True)
    ds = (p * (dp - delta)).astype(BF16)
    dv = mm(p.astype(BF16), ds_)
    dk = mm(ds, qs)
    dq = unstacked(mm(k, ds, TN), own) * (DH ** (-0.5))

    eq = head_spread(pair, 0, RQ, (128, RQ * 128))
    qe = mm(qf_ref[:, :128], eq)
    dq6 = jnp.concatenate([dq] * RQ, axis=1)
    tq_ref[...] += dq6 * qe
    aq_ref[...] += mm((dq6 * bq_ref[...]).astype(BF16), eq, NT)
    ek = head_spread(pair, 0, RK, (128, RK * 128))
    ev = head_spread(pair, KCOLS - 128, RK, (128, RK * 128))
    ke = mm(kvw_ref[:, :128], ek)
    ve = mm(kvw_ref[:, 128:256], ev)
    dk2 = jnp.concatenate([dk] * RK, axis=1)
    dv2 = jnp.concatenate([dv] * RK, axis=1)
    tk_ref[...] += dk2 * ke
    tv_ref[...] += dv2 * ve
    ak_ref[...] += mm((dk2 * bk_ref[...]).astype(BF16), ek, NT)
    av_ref[...] += mm((dv2 * bv_ref[...]).astype(BF16), ev, NT)

    @pl.when(pair == last)
    def _():
        def fold(x, t):
            hi = x.astype(BF16)
            lo = (x - hi.astype(F32)).astype(BF16)
            return mm(hi, t, NT) + mm(lo, t, NT)

        gq = fold(tq_ref[...], rank_tile(QA, (QPAD, RQ * 128)))
        gq_ref[:, :128] = ((gq[:, :128] + aq_ref[...]) * (1.0 / RQ)).astype(BF16)
        gq_ref[:, 128:] = (gq[:, 128:] * (1.0 / RQ)).astype(BF16)
        gk = fold(tk_ref[...], rank_tile(KA, (KPAD, RK * 128)))
        gv = fold(tv_ref[...], rank_tile(KCOLS + KA, (KPAD, RK * 128)))
        gkv = gk + gv
        first = ((gkv[:, :128] + ak_ref[...]) * (1.0 / RK)).astype(BF16)
        second = ((gkv[:, 128:256] + av_ref[...]) * (1.0 / RK)).astype(BF16)
        third = (gkv[:, 256:] * (1.0 / RK)).astype(BF16)
        gkv_ref[...] = jnp.zeros_like(gkv_ref)
        for i in range(nblk):
            rows = slice(i * own, (i + 1) * own)
            slot = s_ref[1 + nblk + i]
            gkv_ref[slot, :, :128] = first[rows]
            gkv_ref[slot, :, 128:256] = second[rows]
            gkv_ref[slot, :, 256:] = third[rows]


def back(nblk, width, scalars, q, k, v, lse, dq, dk, qf, kvw, dn, hm, c, wo, gain):
    own, d = q.shape
    win = nblk * own
    whole = lambda a: pl.BlockSpec(a.shape, lambda p, a=a: (0,) * a.ndim)
    col = lambda rows: pl.BlockSpec((rows, 128), lambda p: (0, p))
    fixed = lambda *s: pl.BlockSpec(s, lambda p: (0,) * len(s))
    return pl.pallas_call(
        functools.partial(back_kernel, nblk),
        grid=(PAIRS,),
        in_specs=[
            pl.BlockSpec(memory_space=pltpu.SMEM), col(own), col(win), col(win),
            pl.BlockSpec((1, 1, 2 * own), lambda p: (p, 0, 0)),
        ] + [whole(a) for a in (dq, dk, qf, kvw, dn, hm, c, wo, gain)],
        out_specs=[
            fixed(own, d), fixed(own, d), fixed(1, d), fixed(own, QPAD),
            fixed(width, own, KPAD),
        ],
        out_shape=[
            jax.ShapeDtypeStruct((own, d), F32),
            jax.ShapeDtypeStruct((own, d), BF16),
            jax.ShapeDtypeStruct((1, d), F32),
            jax.ShapeDtypeStruct((own, QPAD), BF16),
            jax.ShapeDtypeStruct((width, own, KPAD), BF16),
        ],
        scratch_shapes=[
            pltpu.VMEM((own, RQ * 128), F32),
            pltpu.VMEM((win, RK * 128), F32),
            pltpu.VMEM((win, RK * 128), F32),
            pltpu.VMEM((win, own), F32),
            pltpu.VMEM((PAIRS, own, 128), BF16),
            pltpu.VMEM((own, 128), F32),
            pltpu.VMEM((win, 128), F32),
            pltpu.VMEM((win, 128), F32),
            pltpu.VMEM((own, RQ * 128), F32),
            pltpu.VMEM((win, RK * 128), F32),
            pltpu.VMEM((win, RK * 128), F32),
        ],
        compiler_params=params(),
        cost_estimate=cost(30e9, 15e6),
        name="back",
    )(scalars, q, k, v, lse, dq, dk, qf, kvw, dn, hm, c, wo, gain)


def flip(index, bit):
    digit = (index // bit) % 2
    return index + bit - 2 * bit * digit


AXES = {"c": ("wide", 1), "x": ("wide", 2), "y": ("rows", 1), "n": ("rows", 2), "f": ("rows", 4)}


def enter(names):
    barrier = pltpu.get_barrier_semaphore()
    for name in names:
        pl.semaphore_signal(
            barrier, inc=1, device_id=partner(name), device_id_type=pl.DeviceIdType.MESH
        )
    pl.semaphore_wait(barrier, len(names))


def partner(name):
    axis, bit = AXES[name]
    return {axis: flip(lax.axis_index(axis), bit)}


def digit(name):
    axis, bit = AXES[name]
    return (lax.axis_index(axis) // bit) % 2


def wide_digits(index):
    return index // 2, index % 2


def slot_for(me, block):
    mx, mc = wide_digits(me)
    bx, bc = wide_digits(block)
    return 2 * ((mc + bc) % 2) + (mx + bx) % 2


def send_to(name, src, dst, send, recv):
    return pltpu.make_async_remote_copy(
        src_ref=src, dst_ref=dst, send_sem=send, recv_sem=recv,
        device_id=partner(name), device_id_type=pl.DeviceIdType.MESH,
    )


class Gather:
    def __init__(self, ref, send, recv, rows=None):
        at = [ref.at[i] if rows is None else ref.at[i, rows] for i in range(4)]
        self.x = send_to("x", at[0], at[1], send.at[0], recv.at[0])
        self.c = send_to("c", at[0], at[2], send.at[1], recv.at[1])
        self.r = send_to("c", at[1], at[3], send.at[2], recv.at[2])

    def first(self):
        self.x.start()
        self.c.start()

    def relay(self):
        self.x.wait()
        self.r.start()

    def done(self):
        self.c.wait()
        self.r.wait()


class Scatter:
    def __init__(self, part, got, last, send, recv):
        self.part, self.got, self.last = part, got, last
        self.c = send_to("c", part.at[pl.ds(2, 2)], got, send.at[0], recv.at[0])
        if last is not None:
            self.x = send_to("x", part.at[1], last, send.at[1], recv.at[1])

    def core(self):
        self.c.start()

    def kept(self, i):
        return self.part[i].astype(F32) + self.got[i].astype(F32)

    def cross(self):
        self.c.wait()
        self.part[1] = self.kept(1).astype(BF16)
        self.x.start()
        self.part[0] = self.kept(0).astype(BF16)

    def total(self):
        self.x.wait()
        return self.part[0].astype(F32) + self.last[...].astype(F32)


class Sum:
    def __init__(self, names, unit, src, base, acc, got, res, rbase, send, recv,
                 local=None, top=None, flat=False):
        self.names, self.unit, self.n = names, unit, len(names)
        self.src, self.base, self.acc, self.got = src, base, acc, got
        self.res, self.rbase, self.send, self.recv = res, rbase, send, recv
        self.local, self.flat = local, flat
        self.top = unit * 2 ** (self.n - 1) if top is None else top

    def low(self, i, skip=0):
        total = 0
        for j in range(skip, i):
            total = total + digit(self.names[j]) * 2 ** (self.n - 1 - j)
        return total

    def span(self, ref, base, chunk, count):
        return ref.at[pl.ds(base + chunk * self.unit, count * self.unit)]

    def keep(self):
        half = 2 ** (self.n - 1)
        return pltpu.make_async_copy(
            self.span(self.src, self.base, self.low(1), half), self.acc, self.local
        )

    def halve(self, i):
        half = 2 ** (self.n - 1 - i)
        away = (1 - digit(self.names[i])) * half
        if i == 0:
            src = self.span(self.src, self.base, away, half)
        else:
            src = self.span(self.acc, 0, self.low(i, 1) + away, half)
        dst = self.span(self.got, 0, 2 ** self.n - 2 * half, half)
        return send_to(self.names[i], src, dst, self.send.at[i], self.recv.at[i])

    def begin(self):
        self.halve(0).start()
        if self.local is not None:
            self.keep().start()

    def place(self, i):
        if self.flat:
            return self.rbase
        return self.rbase + digit(self.names[0]) * self.top + self.low(i, 1) * self.unit

    def double(self, i):
        half = 2 ** (self.n - 1 - i)
        held = self.res.at[pl.ds(self.place(i + 1), half * self.unit)]
        k = self.n + i
        return send_to(self.names[i], held, held, self.send.at[k], self.recv.at[k])

    def resume(self, own, at):
        place = self.place(self.n)
        for j in range(self.unit):
            self.res[place + j] = own[at + j]
        self.double(self.n - 1).start()

    def add(self, i):
        half = 2 ** (self.n - 1 - i)
        offset = (2 ** self.n - 2 * half) * self.unit
        self.halve(i).wait()
        kept = self.low(i + 1, 1) * self.unit
        first = i == 0 and self.local is None
        if i == 0 and self.local is not None:
            self.keep().wait()
        own = self.base + self.low(1) * self.unit
        last = i == self.n - 1
        place = self.place(self.n)

        count = self.unit if self.unit > 1 else min(half, 4)

        def some(i, carry):
            j = i * count
            mine = self.src[pl.ds(own + j, count)] if first else self.acc[pl.ds(kept + j, count)]
            value = (mine.astype(F32) + self.got[pl.ds(offset + j, count)].astype(F32)).astype(BF16)
            if last:
                self.res[pl.ds(place + j, count)] = value
            else:
                self.acc[pl.ds(kept + j, count)] = value
            return carry

        lax.fori_loop(0, half * self.unit // count, some, 0)

    def step(self, k):
        n = self.n
        if k < n:
            self.add(k)
            if k < n - 1:
                self.halve(k + 1).start()
            elif not self.flat:
                self.double(n - 1).start()
        else:
            i = 2 * n - 1 - k
            self.double(i).wait()
            if i > 0:
                self.double(i - 1).start()


def fill_cap(me, first, dq, dk, cap_ref, nblk, own):
    for i in range(nblk):
        rows = pl.ds(i * own, own)
        key = lax.broadcasted_iota(jnp.int32, (own, own), 0)
        query = lax.broadcasted_iota(jnp.int32, (own, own), 1) + (me - first - i) * own
        ok = (dk[i * own:(i + 1) * own, :] == dq) & (key <= query)
        cap_ref[rows, :] = jnp.where(ok, BIG, NEG)


def fore_kernel(
    nblk, x_ref, wt_ref, wo_ref, g1_ref, g2_ref, dq_ref, dk_ref, c_ref,
    n1_ref, qf_ref, kvw_ref, att_ref, q_ref, k_ref, v_ref, lse_ref, hm_ref, ng_ref, cg_ref,
    kvg_ref, bq_ref, bk_ref, bv_ref, cap_ref, full_ref, send, recv,
):
    seqs, own, d = x_ref.shape
    me = lax.axis_index("wide")
    first = me // 3
    kvs = [Gather(kvg_ref.at[s], send.at[s], recv.at[s]) for s in range(seqs)]
    cots = [Gather(cg_ref.at[s], send.at[2 + s], recv.at[2 + s]) for s in range(seqs)]
    norms = [Gather(ng_ref.at[0], send.at[4], recv.at[4])]
    norms += [
        Gather(ng_ref.at[1], send.at[5 + i], recv.at[5 + i], pl.ds(i * (own // 4), own // 4))
        for i in range(4)
    ]
    for s in range(seqs):
        cg_ref[s, 0] = c_ref[s]
    for s in range(seqs):
        x = x_ref[s].astype(F32)
        r = lax.rsqrt(jnp.mean(x * x, axis=-1, keepdims=True) + EPS)
        n = (x * r * g1_ref[...]).astype(BF16)
        n1_ref[s] = n
        f = mm(n, wt_ref[...], NT).astype(BF16)
        qf_ref[s] = f[:, :QPAD]
        kvg_ref[s, 0, :, :KV] = f[:, QCOLS:]
        kvg_ref[s, 0, :, KV:] = jnp.zeros((own, KPAD - KV), BF16)
        if s == 0:
            enter("cx")
        kvs[s].first()
    kvs[0].relay()
    for s in range(seqs):
        cots[s].first()
    kvs[0].done()

    def step(t, carry):
        s = t // PAIRS
        pair = t % PAIRS

        @pl.when(t == PAIRS)
        def _():
            kvs[1].done()

        @pl.when(pair == 0)
        def _():
            for i in range(nblk):
                kvw_ref[s, pl.ds(i * own, own), :] = kvg_ref[s, slot_for(me, first + i)]
            bq_ref[...] = mm(qf_ref[s], rank_tile(QA, (QPAD, RQ * 128)))
            bk_ref[...] = mm(kvw_ref[s, :, :256], rank_tile(KA, (256, RK * 128)))
            bv_ref[...] = mm(kvw_ref[s, :, 128:384], rank_tile(KCOLS + KA - 128, (256, RK * 128)))
            fill_cap(me, first, dq_ref[s], dk_ref[s], cap_ref, nblk, own)

        qe = mm(qf_ref[s, :, :128], head_spread(pair, 0, RQ, (128, RQ * 128)))
        qsum = qe[:, :128] * bq_ref[:, :128]
        for r in range(1, RQ):
            cols = slice(r * 128, (r + 1) * 128)
            qsum = qsum + qe[:, cols] * bq_ref[:, cols]
        q = (qsum * (1.0 / RQ)).astype(BF16)
        ke = mm(kvw_ref[s, :, :128], head_spread(pair, 0, RK, (128, RK * 128)))
        ve = mm(kvw_ref[s, :, 128:256], head_spread(pair, KCOLS - 128, RK, (128, RK * 128)))
        k = ((ke[:, :128] * bk_ref[:, :128] + ke[:, 128:] * bk_ref[:, 128:]) * (1.0 / RK)).astype(BF16)
        v = ((ve[:, :128] * bv_ref[:, :128] + ve[:, 128:] * bv_ref[:, 128:]) * (1.0 / RK)).astype(BF16)
        q = q * jnp.asarray(DH ** (-0.5), BF16)
        q_ref[s, pair] = q
        k_ref[s, pair] = k
        v_ref[s, pair] = v
        cap = cap_ref[...]
        st = jnp.minimum(mm(k, stacked(q), NT), jnp.concatenate([cap, cap], axis=1))
        top = jnp.max(st, axis=0, keepdims=True)
        e = jnp.exp(st - top)
        total = jnp.sum(e, axis=0, keepdims=True)
        p = (e * (1.0 / total)).astype(BF16)
        lse_ref[s, pair] = top + jnp.log(total)
        full_ref[pair] = unstacked(mm(v, p, TN), own).astype(BF16)

        @pl.when(pair == PAIRS - 1)
        def _():
            att = jnp.concatenate([full_ref[i] for i in range(PAIRS)], axis=1)
            att_ref[s] = att
            hm = x_ref[s].astype(F32) + mm(att, wo_ref[...])
            hm_ref[s] = hm
            r = lax.rsqrt(jnp.mean(hm * hm, axis=-1, keepdims=True) + EPS)
            ng_ref[s, 0] = (hm * r * g2_ref[...]).astype(BF16)

        @pl.when(t == 2)
        def _():
            kvs[1].relay()

        @pl.when(t == 6)
        def _():
            cots[0].relay()

        @pl.when(t == PAIRS - 1)
        def _():
            norms[0].first()

        @pl.when(t == 13)
        def _():
            cots[1].relay()

        return carry

    lax.fori_loop(0, seqs * PAIRS, step, 0)
    for norm in norms[1:]:
        norm.first()
    for norm in norms:
        norm.relay()
    for each in cots + norms:
        each.done()


def vmem():
    return pl.BlockSpec(memory_space=pltpu.VMEM)


def hbm():
    return pl.BlockSpec(memory_space=pl.ANY)


def fused(ident, limit=63):
    return pltpu.CompilerParams(
        vmem_limit_bytes=limit << 20, collective_id=ident, has_side_effects=True
    )


def fore(nblk, x, wt, wo, g1, g2, dq, dk, c):
    seqs, own, d = x.shape
    win = nblk * own
    shape = jax.ShapeDtypeStruct
    return pl.pallas_call(
        functools.partial(fore_kernel, nblk),
        in_specs=[vmem()] * 8,
        out_specs=[vmem()] * 11,
        out_shape=[
            shape((seqs, own, d), BF16), shape((seqs, own, QPAD), BF16),
            shape((seqs, win, KPAD), BF16), shape((seqs, own, d), BF16),
            shape((seqs, PAIRS, own, 128), BF16), shape((seqs, PAIRS, win, 128), BF16),
            shape((seqs, PAIRS, win, 128), BF16), shape((seqs, PAIRS, 1, 2 * own), F32),
            shape((seqs, own, d), F32), shape((seqs, 4, own, d), BF16),
            shape((seqs, 4, own, d), BF16),
        ],
        scratch_shapes=[
            pltpu.VMEM((seqs, 4, own, KPAD), BF16),
            pltpu.VMEM((own, RQ * 128), F32),
            pltpu.VMEM((win, RK * 128), F32),
            pltpu.VMEM((win, RK * 128), F32),
            pltpu.VMEM((win, own), F32),
            pltpu.VMEM((PAIRS, own, 128), BF16),
            pltpu.SemaphoreType.DMA((9, 3)),
            pltpu.SemaphoreType.DMA((9, 3)),
        ],
        compiler_params=fused(0),
        cost_estimate=cost(30e9, 30e6),
        name="fore",
    )(x, wt, wo, g1, g2, dq, dk, c)


SPLITS = ((0, 192), (192, 256), (448, 256))
EARLY = len(SPLITS) - 1
LANES = 512
FFN_NAMES = (("ynf", "ynf", "nyf"), ("ynf", "nyf", "ynf"), ("ynf", "nyf", "ynf"))


def chunk_units(h):
    return SPLITS[h][1] // 16 * (1024 // LANES) // 8


def own_at(h, m):
    return 3 * sum(chunk_units(i) for i in range(h)) + m * chunk_units(h)


MIDDLE_EVENTS = {
    (1, 5): ((0, 0, 0),),
    (1, "m0"): ((0, 2, 0),),
    (1, "m1"): ((0, 1, 0), (0, 0, 1),),
    (2, 1): ((0, 0, 2), (1, 0, 0),),
    (2, 2): ((1, 1, 0), (0, 2, 1),),
    (2, 3): ((0, 1, 1),),
    (2, 5): ((0, 2, 2), (1, 0, 1), (1, 2, 0),),
    (2, 6): ((0, 1, 2),),
    (2, 7): ((1, 1, 1),),
    (2, "m0"): ((1, 0, 2), (1, 2, 1),),
    (2, "m2"): ((1, 1, 2),),
    "end": ((1, 2, 2),),
}


def middle_kernel(
    n_ref, c_ref, wg_ref, wu_ref, wd_ref,
    dn_ref, ds_ref, ok_ref, os_ref, gw_ref, own_ref,
    hid_ref, dg_ref, du_ref, oa_ref, da_ref, op_ref, dp_ref, xs_ref, oc_ref, dc_ref, dx_ref, *refs,
):
    seqs, size, own, d = n_ref.shape
    srcs, refs = refs[:EARLY], refs[EARLY:]
    accs, refs = refs[:3 * EARLY], refs[3 * EARLY:]
    gots, refs = refs[:3 * EARLY], refs[3 * EARLY:]
    send, recv, xsend, xrecv = refs
    downs = [
        send_to("c", dp_ref.at[s], dc_ref.at[s], xsend.at[0, s], xrecv.at[0, s]) for s in range(seqs)
    ]
    ups = [
        send_to("c", op_ref.at[s], oc_ref.at[s], xsend.at[1, s], xrecv.at[1, s]) for s in range(seqs)
    ]
    cross = send_to("x", xs_ref, dx_ref, xsend.at[2, 0], xrecv.at[2, 0])
    parts = {}
    for h in range(EARLY):
        for m in range(3):
            i = 3 * h + m
            u = chunk_units(h)
            parts[h, m] = Sum(
                FFN_NAMES[h][m], u, srcs[h], 8 * u * m, accs[i], gots[i], own_ref, own_at(h, m),
                send.at[i], recv.at[i], flat=True,
            )
    enter("cxynf")

    def run(point):
        for h, m, k in MIDDLE_EVENTS.get(point, ()):
            parts[h, m].step(k)

    for h, (off, rows) in enumerate(SPLITS):
        last = h == EARLY

        def step(t, carry, h=h, off=off, rows=rows, last=last):
            s = t // size
            b = size - 1 - t % size
            n = n_ref[s, b]
            c = c_ref[s, b]
            span = slice(off, off + rows)
            g = mm(wg_ref[span, :], n, NT)
            u = mm(wu_ref[span, :], n, NT)
            dh = mm(wd_ref[span, :], c, NT)
            sg = 1.0 / (1.0 + jnp.exp(-g))
            gs = g * sg
            cols = pl.ds(pl.multiple_of((s * size + b) * own, 128), own)
            hid_ref[span, cols] = (gs * u).astype(BF16)
            dg_ref[span, cols] = (dh * u * (sg * (1.0 + g * (1.0 - sg)))).astype(BF16)
            du_ref[span, cols] = (dh * gs).astype(BF16)
            if last:
                o = mm(hid_ref[:, cols], wd_ref[...], TN)
                dn = mm(dg_ref[:, cols], wg_ref[...], TN) + mm(du_ref[:, cols], wu_ref[...], TN)

                @pl.when(b >= 2)
                def _():
                    op_ref[s, b - 2] = o.astype(BF16)
                    dp_ref[s, b - 2] = dn.astype(BF16)

                @pl.when(b < 2)
                def _():
                    oa_ref[s, b] = o.astype(BF16)
                    da_ref[s, b] = dn

                for i in range(seqs):

                    @pl.when(t == i * size + 1)
                    def _(i=i):
                        downs[i].start()
                        ups[i].start()

                @pl.when(t == size - 1)
                def _():
                    downs[0].wait()
                    xs_ref[...] = (da_ref[0, 1] + dc_ref[0, 1].astype(F32)).astype(BF16)
                    cross.start()

            for j in range(seqs * size):
                if (h, j) in MIDDLE_EVENTS:

                    @pl.when(t == j)
                    def _(j=j):
                        run((h, j))

            return carry

        lax.fori_loop(0, seqs * size, step, 0)
        count = rows // 16
        for m, (a_ref, b_ref) in enumerate(((dg_ref, n_ref), (du_ref, n_ref), (hid_ref, c_ref))):
            w = mm(a_ref[off:off + rows, :], b_ref[...].reshape(seqs * size * own, d)).astype(BF16)
            to = gw_ref if last else srcs[h]
            for i in range(d // LANES):
                at = (m * (d // LANES) + i) * count
                piece = w[:, i * LANES:(i + 1) * LANES]
                to[pl.ds(at, count)] = piece.reshape(count, 16, LANES)
            if not last:
                parts[h, m].begin()
            run((h, "m%d" % m))
    for s in range(seqs):
        ups[s].wait()
        ok_ref[s] = (oa_ref[s, 0].astype(F32) + oc_ref[s, 0].astype(F32)).astype(BF16)
        os_ref[s] = (oa_ref[s, 1].astype(F32) + oc_ref[s, 1].astype(F32)).astype(BF16)
    downs[1].wait()
    dn_ref[1] = da_ref[1, 0] + dc_ref[1, 0].astype(F32)
    ds_ref[...] = (da_ref[1, 1] + dc_ref[1, 1].astype(F32)).astype(BF16)
    run("end")
    cross.wait()
    dn_ref[0] = da_ref[0, 0] + dc_ref[0, 0].astype(F32) + dx_ref[...].astype(F32)


def middle(n, c, wg, wu, wd):
    seqs, size, own, d = n.shape
    shape = jax.ShapeDtypeStruct
    flat = (wd.shape[0], seqs * size * own)
    u = [chunk_units(h) for h in range(EARLY) for _ in range(3)]
    unit = lambda k: pltpu.VMEM((k, 16, LANES), BF16)
    return pl.pallas_call(
        middle_kernel,
        in_specs=[vmem()] * 5,
        out_specs=[vmem()] * 6,
        out_shape=[
            shape((seqs, own, d), F32), shape((own, d), BF16), shape((seqs, own, d), BF16),
            shape((seqs, own, d), BF16), shape((24 * chunk_units(EARLY), 16, LANES), BF16),
            shape((own_at(EARLY, 0), 16, LANES), BF16),
        ],
        scratch_shapes=[pltpu.VMEM(flat, BF16)] * 3
        + [pltpu.VMEM((seqs, 2, own, d), BF16), pltpu.VMEM((seqs, 2, own, d), F32)]
        + [pltpu.VMEM((seqs, 2, own, d), BF16)] * 2
        + [pltpu.VMEM((own, d), BF16)]
        + [pltpu.VMEM((seqs, 2, own, d), BF16)] * 2
        + [pltpu.VMEM((own, d), BF16)]
        + [unit(24 * chunk_units(h)) for h in range(EARLY)]
        + [unit(4 * k) for k in u]
        + [unit(7 * k) for k in u]
        + [
            pltpu.SemaphoreType.DMA((3 * EARLY, 3)),
            pltpu.SemaphoreType.DMA((3 * EARLY, 3)),
            pltpu.SemaphoreType.DMA((3, seqs)),
            pltpu.SemaphoreType.DMA((3, seqs)),
        ],
        compiler_params=fused(1),
        cost_estimate=cost(27e9, 30e6),
        name="middle",
    )(n, c, wg, wu, wd)


FFN_UNITS = 3 * sum(r for _, r in SPLITS) // 16
SECOND = 3
AFTER_EVENTS = {
    0: (("F00", 3), ("F01", 3), ("F20", 0),),
    1: (("F02", 3),),
    2: (("F10", 3), ("F22", 0), ("F11", 3), ("F02", 4), ("F12", 3),),
    4: (("F21", 0), ("O0", 0), ("F11", 4), ("F00", 4), ("O1", 0),),
    5: (("cross", 0), ("F01", 4),),
    6: (("F20", 1), ("F21", 1),),
    7: (("F10", 4), ("O1", 1), ("F22", 1), ("O0", 1),),
    8: (("F20", 2), ("F02", 5), ("F00", 5), ("F21", 2),),
    9: (("cross", 1), ("key", 0), ("F12", 4), ("F22", 2),),
    10: (("F01", 5), ("F20", 3), ("emit", 0),),
    11: (("O0", 2), ("F11", 5), ("F21", 3), ("F10", 5),),
    12: (("F22", 3),),
    13: (("O1", 2), ("F12", 5),),
    14: (("F21", 4),),
    15: (("O1", 3), ("F20", 4), ("emit", 1),),
    "T0": (("O0", 3),),
    "T1": (("F22", 4), ("O1", 4), ("K0", 0), ("K1", 0), ("O0", 4), ("F20", 5), ("O1", 5), ("F21", 5),),
    "T2": (("O0", 5), ("K0", 1), ("K2", 0), ("F22", 5), ("K3", 0), ("K1", 1), ("O1", 6),),
    "T3": (("K4", 0), ("O0", 6), ("K0", 2), ("K2", 1), ("K3", 1), ("O1", 7), ("K1", 2), ("K2", 2), ("K4", 1), ("O0", 7), ("K0", 3), ("K3", 2), ("K2", 3), ("K1", 3), ("K4", 2), ("K0", 4), ("K3", 3), ("K2", 4), ("O1", 8), ("K1", 4), ("K4", 3), ("K3", 4), ("O0", 8), ("K0", 5), ("K1", 5), ("K4", 4), ("K2", 5), ("O1", 9), ("K3", 5), ("K0", 6), ("K4", 5), ("K2", 6), ("O0", 9), ("K1", 6), ("K4", 6), ("K3", 6), ("K0", 7), ("K2", 7), ("K1", 7), ("K3", 7), ("K4", 7), ("K0", 8), ("K3", 8), ("K2", 8), ("K1", 8), ("K0", 9), ("K3", 9), ("K4", 8), ("K2", 9), ("K1", 9), ("K4", 9),),
}
OUT_PARTS = ("cyxnf", "cxnyf")
Q_PARTS = ("cxynf", "cnyfx")
K_PARTS = ("cxynf", "cynfx", "cnfxy")
K_LANES = 256
GAIN_ROW = 352


def attention_parts():
    return [(n, 1024) for n in OUT_PARTS] + [(n, 512) for n in Q_PARTS] + [(n, K_LANES) for n in K_PARTS]


def after_kernel(
    nblk, gw_ref, own_ref, dn_ref, ds_ref, ok_ref, os_ref, q_ref, k_ref, v_ref, lse_ref, dq_ref, dk_ref,
    qf_ref, kvw_ref, hm_ref, c_ref, wo_ref, g1_ref, g2_ref, att_ref, n1_ref, x_ref, wt_ref,
    out_ref, ig_ref, gr_ref, *refs,
):
    n_out, n_q = len(OUT_PARTS), len(Q_PARTS)
    n_fac = n_q + len(K_PARTS)
    or_refs, refs = refs[:n_out], refs[n_out:]
    fr_refs, refs = refs[:n_fac], refs[n_fac:]
    (bq_ref, bk_ref, bv_ref, cap_ref, da_ref, aq_ref, ak_ref, av_ref, tq_ref, tk_ref, tv_ref,
     dm_ref, late_ref, gq_ref, gkp_ref, gkc_ref, gkx_ref, ox_ref, kb_ref, vb_ref, dx_ref, gain_ref) = refs[:22]
    refs = refs[22:]
    gots, refs = refs[:3], refs[3:]
    accs, refs = refs[:3], refs[3:]
    ob, refs = refs[:n_out], refs[n_out:]
    og, refs = refs[:n_out], refs[n_out:]
    oa, refs = refs[:n_out], refs[n_out:]
    fb, refs = refs[:n_fac], refs[n_fac:]
    fg, refs = refs[:n_fac], refs[n_fac:]
    fa, refs = refs[:n_fac], refs[n_fac:]
    send, recv, loc, gs, gr, kvsem, wsem = refs
    seqs, own, d = hm_ref.shape
    me = lax.axis_index("wide")
    first = me // 3

    sums = {}
    half = gr_ref.shape[0] // 2
    for h, (off, rows) in enumerate(SPLITS):
        for m in range(3):
            i = 3 * h + m
            u = chunk_units(h)
            late = h == EARLY
            sums[h, m] = Sum(
                FFN_NAMES[h][m], u, gw_ref if late else None, 8 * u * m,
                accs[m] if late else None, gots[m] if late else None,
                gr_ref, m * (half // 3) + off // 16, send.at[i], recv.at[i],
                local=loc.at[m] if late else None, top=half,
            )
    k0 = len(sums)
    outs = [
        Sum(names, 1, ob[g], 0, oa[g], og[g], or_refs[g], 0, send.at[k0 + g], recv.at[k0 + g])
        for g, names in enumerate(OUT_PARTS)
    ]
    k1 = k0 + n_out
    facs = [
        Sum(names, 1, fb[g], 0, fa[g], fg[g], fr_refs[g], 0, send.at[k1 + g], recv.at[k1 + g])
        for g, names in enumerate(Q_PARTS + K_PARTS)
    ]
    keys = [
        Scatter(gkp_ref.at[s], gkc_ref.at[s], gkx_ref.at[s], gs.at[s], gr.at[s])
        for s in range(seqs)
    ]
    crosses = [
        send_to("x", os_ref.at[s], ox_ref.at[s], gs.at[2 + s, 0], gr.at[2 + s, 0])
        for s in range(seqs)
    ]

    def fetch(t):
        return [
            pltpu.make_async_copy(a.at[t // PAIRS, t % PAIRS], b.at[t % 2], kvsem.at[i, t % 2])
            for i, (a, b) in enumerate(((k_ref, kb_ref), (v_ref, vb_ref)))
        ]

    for copy in fetch(0):
        copy.start()
    loads = [
        pltpu.make_async_copy(dn_ref, dm_ref, wsem.at[0]),
        pltpu.make_async_copy(c_ref, late_ref, wsem.at[1]),
    ]
    for copy in loads:
        copy.start()
    enter("cxynf")
    for h, m in sums:
        if h == EARLY:
            sums[h, m].begin()
        else:
            sums[h, m].resume(own_ref, own_at(h, m))

    for copy in loads:
        copy.wait()
    down = send_to("x", ds_ref, dx_ref, gs.at[4, 0], gr.at[4, 0])
    down.start()
    gain_ref[...] = jnp.zeros((1, d), F32)

    def mids(s):
        hm = hm_ref[s]
        dn = dm_ref[s]
        r = lax.rsqrt(jnp.mean(hm * hm, axis=-1, keepdims=True) + EPS)
        z = dn * g2_ref[...]
        gain_ref[...] += jnp.sum(dn * hm * r, axis=0, keepdims=True)
        dm = (
            late_ref[s].astype(F32)
            + r * z
            - hm * (r * r * r) * jnp.mean(z * hm, axis=-1, keepdims=True)
        )
        dm_ref[s] = dm
        low = dm.astype(BF16)
        late_ref[s] = low
        da = mm(low, wo_ref[...], NT).astype(BF16)
        for i in range(PAIRS):
            da_ref[s, i] = da[:, i * 128:(i + 1) * 128]

    load_x = pltpu.make_async_copy(x_ref, late_ref, wsem.at[2])

    def second():
        for g in range(n_out):

            def rows(j, carry, g=g):
                cols = pl.ds(pl.multiple_of(g * 512 + j * 256, 128), 256)
                a = att_ref[:, :, cols].reshape(seqs * own, 256)
                w = mm(a, late_ref[...].reshape(seqs * own, d), TN).astype(BF16)
                ob[g][pl.ds(j * 16, 16)] = w.reshape(16, 16, d)
                return carry

            lax.fori_loop(0, 2, rows, 0)
            outs[g].begin()
        load_x.start()

    def finish(s):
        def fold(x, t):
            hi = x.astype(BF16)
            lo = (x - hi.astype(F32)).astype(BF16)
            return mm(hi, t, NT) + mm(lo, t, NT)

        gq = fold(tq_ref[...], rank_tile(QA, (QPAD, RQ * 128)))
        gq_ref[s, :, :128] = ((gq[:, :128] + aq_ref[...]) * (1.0 / RQ)).astype(BF16)
        gq_ref[s, :, 128:] = (gq[:, 128:] * (1.0 / RQ)).astype(BF16)
        gk = fold(tk_ref[...], rank_tile(KA, (KPAD, RK * 128)))
        gv = fold(tv_ref[...], rank_tile(KCOLS + KA, (KPAD, RK * 128)))
        gkv = gk + gv
        one = ((gkv[:, :128] + ak_ref[...]) * (1.0 / RK)).astype(BF16)
        two = ((gkv[:, 128:256] + av_ref[...]) * (1.0 / RK)).astype(BF16)
        three = (gkv[:, 256:] * (1.0 / RK)).astype(BF16)
        gkp_ref[s] = jnp.zeros_like(gkp_ref[s])
        for i in range(nblk):
            rows = slice(i * own, (i + 1) * own)
            slot = slot_for(me, first + i)
            gkp_ref[s, slot, :, :128] = one[rows]
            gkp_ref[s, slot, :, 128:256] = two[rows]
            gkp_ref[s, slot, :, 256:] = three[rows]

    def emit(s):
        crosses[s].wait()
        total = hm_ref[s] + (ok_ref[s].astype(F32) + ox_ref[s].astype(F32))
        out_ref[s] = total.astype(BF16)

    named = {"F%d%d" % key: part for key, part in sums.items()}
    named.update({"O%d" % g: part for g, part in enumerate(outs)})
    named.update({"K%d" % g: part for g, part in enumerate(facs)})

    def run(point):
        for name, k in AFTER_EVENTS.get(point, ()):
            if name == "cross":
                crosses[k].start()
            elif name == "emit":
                emit(k)
            elif name == "key":
                keys[k].cross()
            else:
                named[name].step(k)

    def step(t, carry):
        s = t // PAIRS
        pair = t % PAIRS
        slot = t % 2

        @pl.when(t < seqs * PAIRS - 1)
        def _():
            for copy in fetch(t + 1):
                copy.start()

        @pl.when(pair == 0)
        def _():
            bq_ref[...] = mm(qf_ref[s], rank_tile(QA, (QPAD, RQ * 128)))
            bk_ref[...] = mm(kvw_ref[s, :, :256], rank_tile(KA, (256, RK * 128)))
            bv_ref[...] = mm(kvw_ref[s, :, 128:384], rank_tile(KCOLS + KA - 128, (256, RK * 128)))
            fill_cap(me, first, dq_ref[s], dk_ref[s], cap_ref, nblk, own)
            for ref in (aq_ref, ak_ref, av_ref, tq_ref, tk_ref, tv_ref):
                ref[...] = jnp.zeros_like(ref)

        @pl.when(t == SECOND)
        def _():
            down.wait()
            dm_ref[1] += dx_ref[...].astype(F32)

        @pl.when((t == 0) | (t == SECOND))
        def _():
            mids(t // SECOND)

        @pl.when(t == SECOND)
        def _():
            second()

        for copy in fetch(t):
            copy.wait()
        q = q_ref[s, pair]
        k = kb_ref[slot]
        v = vb_ref[slot]
        qs = stacked(q)
        da = stacked(da_ref[s, pair])
        cap = cap_ref[...]
        st = jnp.minimum(mm(k, qs, NT), jnp.concatenate([cap, cap], axis=1))
        p = jnp.exp(st - lse_ref[s, pair])
        dp = mm(v, da, NT)
        delta = jnp.sum(p * dp, axis=0, keepdims=True)
        ds = (p * (dp - delta)).astype(BF16)
        dv = mm(p.astype(BF16), da)
        dk = mm(ds, qs)
        dq = unstacked(mm(k, ds, TN), own) * (DH ** (-0.5))

        eq = head_spread(pair, 0, RQ, (128, RQ * 128))
        qe = mm(qf_ref[s, :, :128], eq)
        dq6 = jnp.concatenate([dq] * RQ, axis=1)
        tq_ref[...] += dq6 * qe
        aq_ref[...] += mm((dq6 * bq_ref[...]).astype(BF16), eq, NT)
        ek = head_spread(pair, 0, RK, (128, RK * 128))
        ev = head_spread(pair, KCOLS - 128, RK, (128, RK * 128))
        ke = mm(kvw_ref[s, :, :128], ek)
        ve = mm(kvw_ref[s, :, 128:256], ev)
        dk2 = jnp.concatenate([dk] * RK, axis=1)
        dv2 = jnp.concatenate([dv] * RK, axis=1)
        tk_ref[...] += dk2 * ke
        tv_ref[...] += dv2 * ve
        ak_ref[...] += mm((dk2 * bk_ref[...]).astype(BF16), ek, NT)
        av_ref[...] += mm((dv2 * bv_ref[...]).astype(BF16), ev, NT)

        @pl.when(pair == PAIRS - 1)
        def _():
            finish(s)

        @pl.when(t == PAIRS - 1)
        def _():
            keys[0].core()

        for when in range(seqs * PAIRS):
            if when in AFTER_EVENTS:

                @pl.when(t == when)
                def _(when=when):
                    run(when)

        return carry

    lax.fori_loop(0, seqs * PAIRS, step, 0)
    keys[1].core()
    n1 = n1_ref[...].reshape(seqs * own, d)
    gq = gq_ref[...].reshape(seqs * own, QPAD)
    w = mm(gq, n1, TN).astype(BF16)
    for g in range(n_q):
        fb[g][...] = w[:, g * 512:(g + 1) * 512].reshape(32, 16, 512)
        facs[g].begin()
    dn1 = mm(gq[:, :QCOLS], wt_ref[:QCOLS, :])
    run("T0")
    keys[1].cross()
    run("T1")
    gkv0 = keys[0].total().astype(BF16)
    gkv = jnp.concatenate([gkv0, keys[1].total().astype(BF16)], axis=0)
    gf = mm(gkv, n1, TN)

    def spread(value, only):
        for g in only:
            for i in range(8):
                for j in range(d // K_LANES):
                    row = 16 * (8 * g + i)
                    piece = value[row:row + 16, j * K_LANES:(j + 1) * K_LANES]
                    fb[n_q + g][4 * i + j] = piece.astype(BF16)
            facs[n_q + g].begin()

    last = len(K_PARTS) - 1
    spread(gf, range(last))
    dn1 = dn1 + mm(gkv[:, :KV], wt_ref[QCOLS:, :])
    load_x.wait()
    hin = late_ref[...].reshape(seqs * own, d).astype(F32)
    r1 = lax.rsqrt(jnp.mean(hin * hin, axis=-1, keepdims=True) + EPS)
    z1 = dn1 * g1_ref[...]
    gain_one = jnp.sum(dn1 * hin * r1, axis=0, keepdims=True)
    gf = jnp.concatenate(
        [gf[:GAIN_ROW], gain_one, gain_ref[...], gf[GAIN_ROW + 2:]], axis=0
    )
    spread(gf, (last,))
    run("T2")
    grad = r1 * z1 - hin * (r1 * r1 * r1) * jnp.mean(z1 * hin, axis=-1, keepdims=True)
    ig_ref[...] = (dm_ref[...].reshape(seqs * own, d) + grad).astype(BF16).reshape(seqs, own, d)
    run("T3")


def after(nblk, gw, own_sums, dn, ds, ok, os, q, k, v, lse, dq, dk, qf, kvw, hm, c, wo, g1, g2, att, n1, x, wt):
    seqs, own, d = hm.shape
    win = nblk * own
    shape = jax.ShapeDtypeStruct
    far = (0, 2, 3, 5, 7, 8, 15, 21)
    results = [shape((32, 16, lanes), BF16) for _, lanes in attention_parts()]
    total = 3 * len(SPLITS) + len(results)
    args = (gw, own_sums, dn, ds, ok, os, q, k, v, lse, dq, dk, qf, kvw, hm, c, wo, g1, g2, att, n1, x, wt)
    res = pl.pallas_call(
        functools.partial(after_kernel, nblk),
        in_specs=[hbm() if i in far else vmem() for i in range(len(args))],
        out_specs=[vmem()] * (3 + len(results)),
        out_shape=[
            shape((seqs, own, d), BF16), shape((seqs, own, d), BF16),
            shape((2 * FFN_UNITS, 16, LANES), BF16),
        ] + results,
        scratch_shapes=[
            pltpu.VMEM((own, RQ * 128), F32),
            pltpu.VMEM((win, RK * 128), F32),
            pltpu.VMEM((win, RK * 128), F32),
            pltpu.VMEM((win, own), F32),
            pltpu.VMEM((seqs, PAIRS, own, 128), BF16),
            pltpu.VMEM((own, 128), F32),
            pltpu.VMEM((win, 128), F32),
            pltpu.VMEM((win, 128), F32),
            pltpu.VMEM((own, RQ * 128), F32),
            pltpu.VMEM((win, RK * 128), F32),
            pltpu.VMEM((win, RK * 128), F32),
            pltpu.VMEM((seqs, own, d), F32),
            pltpu.VMEM((seqs, own, d), BF16),
            pltpu.VMEM((seqs, own, QPAD), BF16),
            pltpu.VMEM((seqs, 4, own, KPAD), BF16),
            pltpu.VMEM((seqs, 2, own, KPAD), BF16),
            pltpu.VMEM((seqs, own, KPAD), BF16),
            pltpu.VMEM((seqs, own, d), BF16),
            pltpu.VMEM((2, win, 128), BF16),
            pltpu.VMEM((2, win, 128), BF16),
            pltpu.VMEM((own, d), BF16),
            pltpu.VMEM((1, d), F32),
        ]
        + [pltpu.VMEM((7 * chunk_units(EARLY), 16, LANES), BF16)] * 3
        + [pltpu.VMEM((4 * chunk_units(EARLY), 16, LANES), BF16)] * 3
        + [pltpu.VMEM((n, 16, 1024), BF16) for n in (32, 31, 16) for _ in OUT_PARTS]
        + [
            pltpu.VMEM((n, 16, lanes), BF16) for n in (32, 31, 16)
            for _, lanes in attention_parts()[len(OUT_PARTS):]
        ]
        + [
            pltpu.SemaphoreType.DMA((total, 10)),
            pltpu.SemaphoreType.DMA((total, 10)),
            pltpu.SemaphoreType.DMA((3,)),
            pltpu.SemaphoreType.DMA((5, 2)),
            pltpu.SemaphoreType.DMA((5, 2)),
            pltpu.SemaphoreType.DMA((2, 2)),
            pltpu.SemaphoreType.DMA((3,)),
        ],
        compiler_params=fused(2),
        cost_estimate=cost(60e9, 60e6),
        name="after",
    )(*args)
    n = 3 + len(OUT_PARTS)
    return res[0], res[1], res[2], res[3:n], res[n:]


def last_kernel(
    out_ref, ig_ref, gr_ref, o0_ref, o1_ref, q0_ref, q1_ref, k0_ref, k1_ref, k2_ref,
    output_ref, grad_ref, gate_ref, up_ref, down_ref, go_ref, gf_ref, gain_ref,
):
    step = pl.program_id(0)
    output_ref[...] = out_ref[...]
    grad_ref[...] = ig_ref[...]
    units = gr_ref.shape[2]
    for m, ref in enumerate((gate_ref, up_ref, down_ref)):
        for i in range(2):
            ref[:, i * LANES:(i + 1) * LANES] = gr_ref[i, m].reshape(16 * units, LANES).astype(F32)
    for g, ref in enumerate((o0_ref, o1_ref)):

        @pl.when(step // 2 == g)
        def _(ref=ref):
            half = pl.ds((step % 2) * 16, 16)
            go_ref[...] = ref[half].reshape(256, 1024).astype(F32)

    rows = pl.ds(pl.multiple_of(step * 128, 128), 128)
    for i, ref in enumerate((q0_ref, q1_ref)):
        gf_ref[rows, i * 512:(i + 1) * 512] = ref[pl.ds(step * 8, 8)].reshape(128, 512).astype(F32)

    @pl.when(step == 3)
    def _():
        for g, ref in enumerate((k0_ref, k1_ref, k2_ref)):
            count = min(KV - 128 * g, 128) // 16

            def rows(i, carry, g=g, ref=ref):
                at = pl.ds(pl.multiple_of(QCOLS + 128 * g + 16 * i, 16), 16)
                for j in range(1024 // K_LANES):
                    cols = slice(j * K_LANES, (j + 1) * K_LANES)
                    gf_ref[at, cols] = ref[4 * i + j].astype(F32)
                return carry

            lax.fori_loop(0, count, rows, 0)
        unit = (GAIN_ROW - 256) // 16
        for j in range(1024 // K_LANES):
            cols = slice(j * K_LANES, (j + 1) * K_LANES)
            gain_ref[:, cols] = k2_ref[4 * unit + j].astype(F32)[:8]


def finish_all(output, grad, gr, go, gf, cols):
    seqs, own, d = output.shape
    ff = 16 * gr.shape[0] // 6
    gr = gr.reshape(2, 3, ff // 16, 16, LANES)
    steps = 4
    shape = jax.ShapeDtypeStruct
    whole = lambda a: pl.BlockSpec(a.shape, lambda i, a=a: (0,) * len(a.shape))
    tokens = pl.BlockSpec((seqs, own // steps, d), lambda i: (0, i, 0))
    outs = [
        shape(output.shape, BF16), shape(output.shape, BF16), shape((ff, d), F32),
        shape((ff, d), F32), shape((ff, d), F32), shape((d, d), F32), shape((cols, d), F32),
        shape((8, d), F32),
    ]
    rows = lambda n: pl.BlockSpec((n // steps, d), lambda i: (i, 0))
    return pl.pallas_call(
        last_kernel,
        grid=(steps,),
        in_specs=[
            tokens, tokens,
            pl.BlockSpec((2, 3, ff // 16 // steps, 16, LANES), lambda i: (0, 0, i, 0, 0)),
        ] + [whole(a) for a in list(go) + list(gf)],
        out_specs=[tokens, tokens, rows(ff), rows(ff), rows(ff), rows(d), whole(outs[6]), whole(outs[7])],
        out_shape=outs,
        compiler_params=params(),
        cost_estimate=cost(1e6, 30e6),
        name="last",
    )(output, grad, gr, *go, *gf)


def fused_body(
    tokens, doc_ids, factor_weight, output_weight, norm_one, norm_two,
    gate_weight, up_weight, down_weight, cotangent,
):
    seqs, own, d = tokens.shape
    me = lax.axis_index("wide")
    nblk = -(-(MAX_DOC - 1) // own) + 1
    first = me // 3
    g1 = norm_one[None]
    g2 = norm_two[None]
    dq = lax.dynamic_slice_in_dim(doc_ids, me * own, own, 1)[:, None, :]
    dk = lax.dynamic_slice_in_dim(doc_ids, first * own, nblk * own, 1)[:, :, None]
    wt = factor_weight.T
    n1, qf, kvw, att, q, k, v, lse, hm, ng, cg = fore(
        nblk, tokens, wt, output_weight, g1, g2, dq, dk, cotangent
    )
    dn, ds, ok, os, gw, own_sums = middle(ng, cg, gate_weight.T, up_weight.T, down_weight)
    output, input_grad, gr, go, gf = after(
        nblk, gw, own_sums, dn, ds, ok, os, q, k, v, lse, dq, dk, qf, kvw, hm, cotangent, output_weight,
        g1, g2, att, n1, tokens, wt,
    )
    output, input_grad, gate, up, down, out, fac, gain = finish_all(
        output, input_grad, gr, go, gf, factor_weight.shape[1]
    )
    return output, input_grad, fac.T, out, gain[0], gain[1], gate.T, up.T, down


def swap(x, axis, size, bit):
    return lax.ppermute(x, axis, [(i, i ^ bit) for i in range(size)])


def steps_of(size):
    bits, b = [], size // 2
    while b:
        bits.append(b)
        b //= 2
    return bits


def gather(x, size):
    buf = x[None]
    for bit in steps_of(size):
        buf = jnp.concatenate([buf, swap(buf, "wide", size, bit)], axis=0)
    return buf


def order_of(size):
    order = [0]
    for bit in steps_of(size):
        order = order + [o ^ bit for o in order]
    return order


def scatter(parts, size):
    for bit in reversed(steps_of(size)):
        half = parts.shape[0] // 2
        got = swap(parts[half:], "wide", size, bit)
        total = parts[:half].astype(F32) + got.astype(F32)
        parts = total if half == 1 else total.astype(BF16)
    return parts[0]


def body(
    tokens, doc_ids, factor_weight, output_weight, norm_one, norm_two,
    gate_weight, up_weight, down_weight, cotangent,
):
    seqs, own, d = tokens.shape
    full_len = doc_ids.shape[1]
    size = full_len // own
    me = lax.axis_index("wide")
    left = min(-(-(MAX_DOC - 1) // own), size - 1)
    nblk = left + 1
    start = jnp.maximum(me - left, 0)
    order = order_of(size)
    slot_of = [order.index(j) for j in range(size)]
    slots = jnp.asarray(slot_of, jnp.int32)
    blocks = start + jnp.arange(nblk, dtype=jnp.int32)
    scalars = jnp.concatenate(
        [me[None].astype(jnp.int32), (me - blocks) * own, slots[me ^ blocks]]
    ).astype(jnp.int32)
    g1 = norm_one[None]
    g2 = norm_two[None]

    n1, qf, kvf = front(tokens.reshape(seqs * own, d), factor_weight, g1)
    qf = qf.reshape(seqs, own, QPAD)
    kvg = gather(kvf.reshape(seqs, own, KPAD), size)
    doc_query = lax.dynamic_slice_in_dim(doc_ids, me * own, own, 1)
    doc_key = lax.dynamic_slice_in_dim(doc_ids, start * own, nblk * own, 1)
    cots = [gather(cotangent[s], size) for s in range(seqs)]

    fwd = []
    for s in range(seqs):
        dq = doc_query[s][None, :]
        dk = doc_key[s][:, None]
        fwd.append(
            (dq, dk)
            + tuple(attend(nblk, scalars, qf[s], kvg[:, s], dq, dk, tokens[s], output_weight, g2))
        )
    prev = None
    outs, dns = [], []
    for s in range(seqs):
        n2 = gather(fwd[s][8], size)
        res = ffn(n2, cots[s], gate_weight, up_weight, down_weight, prev, s == seqs - 1)
        outs.append(res[0])
        dns.append(res[1])
        prev = res[2:]
    grads = [lax.psum(g, "rows").astype(F32) for g in prev]

    output, mids, lows, gain_two, gqs, gkvs = [], [], [], 0.0, [], []
    for s in range(seqs):
        dq, dk, att, q, k, v, lse, hm, n2, kvw = fwd[s]
        dn = scatter(dns[s], size)
        dm, low, gain, gq, gkv = back(
            nblk, size, scalars, q, k, v, lse, dq, dk, qf[s], kvw, dn, hm,
            cotangent[s], output_weight, g2,
        )
        output.append((hm + scatter(outs[s], size)).astype(BF16))
        mids.append(dm)
        lows.append(low)
        gqs.append(gq)
        gkvs.append(gkv)
        gain_two = gain_two + gain
    att_all = jnp.stack([f[2] for f in fwd]).reshape(seqs * own, d)
    grad_out = mm(att_all, jnp.stack(lows).reshape(seqs * own, d), TN)
    gkv = scatter(jnp.stack(gkvs, axis=1), size).astype(BF16)
    dfac = jnp.concatenate([jnp.stack(gqs)[..., :QCOLS], gkv[..., :KV]], axis=-1)
    dfac = dfac.reshape(seqs * own, -1)
    grad_factors = mm(n1, dfac, TN)
    dn1 = mm(dfac, factor_weight, NT)
    hin = tokens.reshape(seqs * own, d).astype(F32)
    r1 = lax.rsqrt(jnp.mean(hin * hin, axis=-1, keepdims=True) + EPS)
    z1 = dn1 * g1
    gain_one = jnp.sum(dn1 * hin * r1, axis=0)
    grad_norm = r1 * z1 - hin * (r1 * r1 * r1) * jnp.mean(z1 * hin, axis=-1, keepdims=True)
    input_grad = (jnp.stack(mids).reshape(seqs * own, d) + grad_norm).astype(BF16)
    parts = [grad_out, grad_factors.T, gain_one[None], gain_two]
    packed = jnp.concatenate([p.astype(BF16) for p in parts], axis=0)
    packed = lax.psum(packed, ("rows", "wide")).astype(F32)
    fac = grad_factors.shape[1]
    return (
        jnp.stack(output),
        input_grad.reshape(seqs, own, d),
        packed[d:d + fac].T,
        packed[:d],
        packed[d + fac],
        packed[d + fac + 1],
        grads[0],
        grads[1],
        grads[2],
    )


def solution(mesh):
    placed = (
        P("rows", "wide", None), P("rows", None), P(), P(), P(), P(),
        P(None, "wide"), P(None, "wide"), P("wide", None), P("rows", "wide", None),
    )
    small = mesh.shape["rows"] == 8 and mesh.shape["wide"] == 4
    return jax.shard_map(
        fused_body if small else body,
        mesh=mesh,
        in_specs=placed,
        out_specs=(
            P("rows", "wide", None), P("rows", "wide", None), P(), P(), P(), P(),
            P(None, "wide"), P(None, "wide"), P("wide", None),
        ),
        check_vma=False,
    )
```

profile of v0, /device:TPU:0, one launch (start us, length us, event | category | flops | bytes accessed | tf_op | source)
XLA Modules:
  0.0 263.7 jit_solution(12290158555295201510)
XLA Ops:
  0.6 0.0 copy-start
  0.7 0.7 copy-done
  1.3 0.6 broadcast_in_dim.14.dq_ref
  1.9 1.2 copy.19.dk_ref
  3.1 70.4 %fore.1 = (bf16[2,256,1024]{2,1,0:T(8,128)(2,1)}, bf16[2,256,512]{2,1,0:T(8,128)(2,1)}, bf16[2,768,384]{2,1,0:T(8,128)(2,1)}, bf16[2,256,1024]{2,1,0:T(8,128)(2,...) custom-call(bf16[2,256,1024]{2,1,0:T(8,128)(2,1)} %x_ref.3, ...), custom_call_target="tpu_custom_call" | custom-call | flops 30000001024 | bytes 30000000 | tf_op jit(solution)/shard_map/fore/pallas_call | solution.py:768
  73.5 58.9 %middle.1 = (f32[2,256,1024]{2,1,0:T(8,128)}, bf16[256,1024]{1,0:T(8,128)(2,1)}, bf16[2,256,1024]{2,1,0:T(8,128)(2,1)}, bf16[2,256,1024]{2,1,0:T(8,128)(2,1)}, b...) custom-call(bf16[2,4,256,1024]{3,2,1,0:T(8,128)(2,1)} %get-tuple-element.44.n_ref, ...), custom_call_target="tpu_custom_call" | custom-call | flops 27000000512 | bytes 30000000 | tf_op jit(solution)/shard_map/middle/pallas_call | solution.py:942
  132.5 119.0 %after.1 = (bf16[2,256,1024]{2,1,0:T(8,128)(2,1)}, bf16[2,256,1024]{2,1,0:T(8,128)(2,1)}, bf16[264,16,512]{2,1,0:T(8,128)(2,1)}, bf16[32,16,1024]{2,1,0:T(8,128)...) custom-call(bf16[96,16,512]{2,1,0:T(8,128)(2,1)} %get-tuple-element., ...), custom_call_target="tpu_custom_call" | custom-call | flops 60000002048 | bytes 60000000 | tf_op jit(solution)/shard_map/after/pallas_call | solution.py:1300
  251.5 0.0 copy-start.1
  251.5 10.7 %last.1 = (bf16[2,256,1024]{2,1,0:T(8,128)(2,1)}, bf16[2,256,1024]{2,1,0:T(8,128)(2,1)}, f32[704,1024]{1,0:T(8,128)}, f32[704,1024]{1,0:T(8,128)}, f32[704,1024]...) custom-call(bf16[2,256,1024]{2,1,0:T(8,128)(2,1)} %get-tuple-element.61.out_ref, ...), custom_call_target="tpu_custom_call" | custom-call | flops 1000000 | bytes 30000000 | tf_op jit(solution)/shard_map/last/pallas_call | solution.py:1411
  262.2 1.4 fusion
  263.7 0.0 copy-done.1
  (2 shorter events, 0.0 us)
Async XLA Ops:
  0.6 0.7 copy-start
  251.5 12.2 %copy-start.1 = (s32[2,1024]{1,0:T(2,128)S(1)}, s32[2,1024]{1,0:T(2,128)}, u32[]{:S(2)}) copy-start(s32[2,1024]{1,0:T(2,128)} %param.11) | copy-start | bytes 24580
where the time goes:
time: 264 us
  Pallas kernels  259 us (98%)
  local copies, waits for them, and re-layouts  3.88 us (1%)
    pallas_call x1, Pallas kernels, after(): pl.pallas_call(functools.partial(after_kernel, nblk), in_specs=[hbm() if...  119 us
    pallas_call x1, Pallas kernels, fore(): pl.pallas_call(functools.partial(fore_kernel, nblk), in_specs=[vmem()] *...  70.4 us
    pallas_call x1, Pallas kernels, middle(): pl.pallas_call(middle_kernel, in_specs=[vmem()] * 5, out_specs=[vmem()] *...  58.9 us
    pallas_call x1, Pallas kernels, finish_all(): pl.pallas_call(last_kernel, grid=(steps,), in_specs=[tokens, tokens, pl.B...  10.7 us

commit v1 on v0

--- a/solution.py
+++ b/solution.py
@@ -639,7 +639,7 @@
 
 def fore_kernel(
     nblk, x_ref, wt_ref, wo_ref, g1_ref, g2_ref, dq_ref, dk_ref, c_ref,
-    n1_ref, qf_ref, kvw_ref, att_ref, q_ref, k_ref, v_ref, lse_ref, hm_ref, ng_ref, cg_ref,
+    n1_ref, qf_ref, kvw_ref, att_ref, q_ref, k_ref, v_ref, lse_ref, hm_ref, ng_ref, nb_ref, cg_ref,
     kvg_ref, bq_ref, bk_ref, bv_ref, cap_ref, full_ref, send, recv,
 ):
     seqs, own, d = x_ref.shape
@@ -647,11 +647,7 @@
     first = me // 3
     kvs = [Gather(kvg_ref.at[s], send.at[s], recv.at[s]) for s in range(seqs)]
     cots = [Gather(cg_ref.at[s], send.at[2 + s], recv.at[2 + s]) for s in range(seqs)]
-    norms = [Gather(ng_ref.at[0], send.at[4], recv.at[4])]
-    norms += [
-        Gather(ng_ref.at[1], send.at[5 + i], recv.at[5 + i], pl.ds(i * (own // 4), own // 4))
-        for i in range(4)
-    ]
+    norm = Gather(ng_ref, send.at[4], recv.at[4])
     for s in range(seqs):
         cg_ref[s, 0] = c_ref[s]
     for s in range(seqs):
@@ -718,7 +714,16 @@
             hm = x_ref[s].astype(F32) + mm(att, wo_ref[...])
             hm_ref[s] = hm
             r = lax.rsqrt(jnp.mean(hm * hm, axis=-1, keepdims=True) + EPS)
-            ng_ref[s, 0] = (hm * r * g2_ref[...]).astype(BF16)
+            n2 = (hm * r * g2_ref[...]).astype(BF16)
+
+            @pl.when(s == 0)
+            def _():
+                ng_ref[0] = n2
+                norm.first()
+
+            @pl.when(s == 1)
+            def _():
+                nb_ref[...] = n2
 
         @pl.when(t == 2)
         def _():
@@ -728,10 +733,6 @@
         def _():
             cots[0].relay()
 
-        @pl.when(t == PAIRS - 1)
-        def _():
-            norms[0].first()
-
         @pl.when(t == 13)
         def _():
             cots[1].relay()
@@ -739,11 +740,8 @@
         return carry
 
     lax.fori_loop(0, seqs * PAIRS, step, 0)
-    for norm in norms[1:]:
-        norm.first()
-    for norm in norms:
-        norm.relay()
-    for each in cots + norms:
+    norm.relay()
+    for each in cots + [norm]:
         each.done()
 
 
@@ -768,13 +766,13 @@
     return pl.pallas_call(
         functools.partial(fore_kernel, nblk),
         in_specs=[vmem()] * 8,
-        out_specs=[vmem()] * 11,
+        out_specs=[vmem()] * 12,
         out_shape=[
             shape((seqs, own, d), BF16), shape((seqs, own, QPAD), BF16),
             shape((seqs, win, KPAD), BF16), shape((seqs, own, d), BF16),
             shape((seqs, PAIRS, own, 128), BF16), shape((seqs, PAIRS, win, 128), BF16),
             shape((seqs, PAIRS, win, 128), BF16), shape((seqs, PAIRS, 1, 2 * own), F32),
-            shape((seqs, own, d), F32), shape((seqs, 4, own, d), BF16),
+            shape((seqs, own, d), F32), shape((4, own, d), BF16), shape((own, d), BF16),
             shape((seqs, 4, own, d), BF16),
         ],
         scratch_shapes=[
@@ -784,8 +782,8 @@
             pltpu.VMEM((win, RK * 128), F32),
             pltpu.VMEM((win, own), F32),
             pltpu.VMEM((PAIRS, own, 128), BF16),
-            pltpu.SemaphoreType.DMA((9, 3)),
-            pltpu.SemaphoreType.DMA((9, 3)),
+            pltpu.SemaphoreType.DMA((5, 3)),
+            pltpu.SemaphoreType.DMA((5, 3)),
         ],
         compiler_params=fused(0),
         cost_estimate=cost(30e9, 30e6),
@@ -794,7 +792,7 @@
 
 
 SPLITS = ((0, 192), (192, 256), (448, 256))
-EARLY = len(SPLITS) - 1
+EARLY = len(SPLITS) - 2
 LANES = 512
 FFN_NAMES = (("ynf", "ynf", "nyf"), ("ynf", "nyf", "ynf"), ("ynf", "nyf", "ynf"))
 
@@ -803,36 +801,35 @@
     return SPLITS[h][1] // 16 * (1024 // LANES) // 8
 
 
+def late_at(h):
+    return 24 * sum(chunk_units(i) for i in range(EARLY, h))
+
+
 def own_at(h, m):
     return 3 * sum(chunk_units(i) for i in range(h)) + m * chunk_units(h)
 
 
 MIDDLE_EVENTS = {
-    (1, 5): ((0, 0, 0),),
-    (1, "m0"): ((0, 2, 0),),
-    (1, "m1"): ((0, 1, 0), (0, 0, 1),),
-    (2, 1): ((0, 0, 2), (1, 0, 0),),
-    (2, 2): ((1, 1, 0), (0, 2, 1),),
-    (2, 3): ((0, 1, 1),),
-    (2, 5): ((0, 2, 2), (1, 0, 1), (1, 2, 0),),
-    (2, 6): ((0, 1, 2),),
-    (2, 7): ((1, 1, 1),),
-    (2, "m0"): ((1, 0, 2), (1, 2, 1),),
-    (2, "m2"): ((1, 1, 2),),
-    "end": ((1, 2, 2),),
+    (1, "m0"): ((0, 0, 0),),
+    (1, "m1"): ((0, 2, 0),),
+    (1, "m2"): ((0, 1, 0), (0, 0, 1),),
+    (2, 0): ((0, 2, 1),),
+    (2, 1): ((0, 1, 1), (0, 0, 2),),
+    (2, 2): ((0, 2, 2),),
+    (2, 3): ((0, 1, 2),),
 }
 
 
 def middle_kernel(
-    n_ref, c_ref, wg_ref, wu_ref, wd_ref,
+    n_ref, nb_ref, c_ref, wg_ref, wu_ref, wd_ref,
     dn_ref, ds_ref, ok_ref, os_ref, gw_ref, own_ref,
-    hid_ref, dg_ref, du_ref, oa_ref, da_ref, op_ref, dp_ref, xs_ref, oc_ref, dc_ref, dx_ref, *refs,
+    hid_ref, dg_ref, du_ref, oa_ref, da_ref, op_ref, dp_ref, xs_ref, oc_ref, dc_ref, dx_ref, nn_ref, *refs,
 ):
-    seqs, size, own, d = n_ref.shape
+    seqs, size, own, d = c_ref.shape
     srcs, refs = refs[:EARLY], refs[EARLY:]
     accs, refs = refs[:3 * EARLY], refs[3 * EARLY:]
     gots, refs = refs[:3 * EARLY], refs[3 * EARLY:]
-    send, recv, xsend, xrecv = refs
+    send, recv, xsend, xrecv, nsend, nrecv = refs
     downs = [
         send_to("c", dp_ref.at[s], dc_ref.at[s], xsend.at[0, s], xrecv.at[0, s]) for s in range(seqs)
     ]
@@ -849,58 +846,84 @@
                 FFN_NAMES[h][m], u, srcs[h], 8 * u * m, accs[i], gots[i], own_ref, own_at(h, m),
                 send.at[i], recv.at[i], flat=True,
             )
+    norms = [
+        Gather(nn_ref, nsend.at[i], nrecv.at[i], pl.ds(i * (own // 4), own // 4)) for i in range(4)
+    ]
+    nn_ref[0] = nb_ref[...]
     enter("cxynf")
+    for norm in norms:
+        norm.first()
 
     def run(point):
         for h, m, k in MIDDLE_EVENTS.get(point, ()):
             parts[h, m].step(k)
 
+    def hidden(s, b, n, span):
+        c = c_ref[s, b]
+        g = mm(wg_ref[span, :], n, NT)
+        u = mm(wu_ref[span, :], n, NT)
+        dh = mm(wd_ref[span, :], c, NT)
+        sg = 1.0 / (1.0 + jnp.exp(-g))
+        gs = g * sg
+        cols = pl.ds(pl.multiple_of((s * size + b) * own, 128), own)
+        hid_ref[span, cols] = (gs * u).astype(BF16)
+        dg_ref[span, cols] = (dh * u * (sg * (1.0 + g * (1.0 - sg)))).astype(BF16)
+        du_ref[span, cols] = (dh * gs).astype(BF16)
+
+    def project(s, b, t):
+        cols = pl.ds(pl.multiple_of((s * size + b) * own, 128), own)
+        o = mm(hid_ref[:, cols], wd_ref[...], TN)
+        dn = mm(dg_ref[:, cols], wg_ref[...], TN) + mm(du_ref[:, cols], wu_ref[...], TN)
+
+        @pl.when(b >= 2)
+        def _():
+            op_ref[s, b - 2] = o.astype(BF16)
+            dp_ref[s, b - 2] = dn.astype(BF16)
+
+        @pl.when(b < 2)
+        def _():
+            oa_ref[s, b] = o.astype(BF16)
+            da_ref[s, b] = dn
+
+        @pl.when(t == 1)
+        def _():
+            downs[s].start()
+            ups[s].start()
+
+    def one(t, carry):
+        b = size - 1 - t
+        hidden(0, b, n_ref[b], slice(0, wd_ref.shape[0]))
+        project(0, b, t)
+
+        @pl.when(t == 1)
+        def _():
+            norms[0].relay()
+
+        @pl.when(t == 2)
+        def _():
+            norms[1].relay()
+            norms[2].relay()
+
+        return carry
+
+    lax.fori_loop(0, size, one, 0)
+    norms[3].relay()
+    downs[0].wait()
+    xs_ref[...] = (da_ref[0, 1] + dc_ref[0, 1].astype(F32)).astype(BF16)
+    cross.start()
+    for norm in norms:
+        norm.done()
+    half = size * own
     for h, (off, rows) in enumerate(SPLITS):
-        last = h == EARLY
-
-        def step(t, carry, h=h, off=off, rows=rows, last=last):
-            s = t // size
-            b = size - 1 - t % size
-            n = n_ref[s, b]
-            c = c_ref[s, b]
-            span = slice(off, off + rows)
-            g = mm(wg_ref[span, :], n, NT)
-            u = mm(wu_ref[span, :], n, NT)
-            dh = mm(wd_ref[span, :], c, NT)
-            sg = 1.0 / (1.0 + jnp.exp(-g))
-            gs = g * sg
-            cols = pl.ds(pl.multiple_of((s * size + b) * own, 128), own)
-            hid_ref[span, cols] = (gs * u).astype(BF16)
-            dg_ref[span, cols] = (dh * u * (sg * (1.0 + g * (1.0 - sg)))).astype(BF16)
-            du_ref[span, cols] = (dh * gs).astype(BF16)
+        last = h == len(SPLITS) - 1
+        early = h < EARLY
+
+        def two(t, carry, h=h, off=off, rows=rows, last=last):
+            b = size - 1 - t
+            hidden(1, b, nn_ref[b], slice(off, off + rows))
             if last:
-                o = mm(hid_ref[:, cols], wd_ref[...], TN)
-                dn = mm(dg_ref[:, cols], wg_ref[...], TN) + mm(du_ref[:, cols], wu_ref[...], TN)
-
-                @pl.when(b >= 2)
-                def _():
-                    op_ref[s, b - 2] = o.astype(BF16)
-                    dp_ref[s, b - 2] = dn.astype(BF16)
-
-                @pl.when(b < 2)
-                def _():
-                    oa_ref[s, b] = o.astype(BF16)
-                    da_ref[s, b] = dn
-
-                for i in range(seqs):
-
-                    @pl.when(t == i * size + 1)
-                    def _(i=i):
-                        downs[i].start()
-                        ups[i].start()
-
-                @pl.when(t == size - 1)
-                def _():
-                    downs[0].wait()
-                    xs_ref[...] = (da_ref[0, 1] + dc_ref[0, 1].astype(F32)).astype(BF16)
-                    cross.start()
-
-            for j in range(seqs * size):
+                project(1, b, t)
+            for j in range(size):
                 if (h, j) in MIDDLE_EVENTS:
 
                     @pl.when(t == j)
@@ -909,16 +932,21 @@
 
             return carry
 
-        lax.fori_loop(0, seqs * size, step, 0)
+        lax.fori_loop(0, size, two, 0)
         count = rows // 16
-        for m, (a_ref, b_ref) in enumerate(((dg_ref, n_ref), (du_ref, n_ref), (hid_ref, c_ref))):
-            w = mm(a_ref[off:off + rows, :], b_ref[...].reshape(seqs * size * own, d)).astype(BF16)
-            to = gw_ref if last else srcs[h]
+        span = slice(off, off + rows)
+        for m, (a_ref, b_refs) in enumerate((
+            (dg_ref, (n_ref, nn_ref)), (du_ref, (n_ref, nn_ref)),
+            (hid_ref, (c_ref.at[0], c_ref.at[1])),
+        )):
+            w = mm(a_ref[span, :half], b_refs[0][...].reshape(half, d))
+            w = (w + mm(a_ref[span, half:], b_refs[1][...].reshape(half, d))).astype(BF16)
+            to, start = (srcs[h], 0) if early else (gw_ref, late_at(h))
             for i in range(d // LANES):
-                at = (m * (d // LANES) + i) * count
+                at = start + (m * (d // LANES) + i) * count
                 piece = w[:, i * LANES:(i + 1) * LANES]
                 to[pl.ds(at, count)] = piece.reshape(count, 16, LANES)
-            if not last:
+            if early:
                 parts[h, m].begin()
             run((h, "m%d" % m))
     for s in range(seqs):
@@ -933,19 +961,19 @@
     dn_ref[0] = da_ref[0, 0] + dc_ref[0, 0].astype(F32) + dx_ref[...].astype(F32)
 
 
-def middle(n, c, wg, wu, wd):
-    seqs, size, own, d = n.shape
+def middle(n, nb, c, wg, wu, wd):
+    seqs, size, own, d = c.shape
     shape = jax.ShapeDtypeStruct
     flat = (wd.shape[0], seqs * size * own)
     u = [chunk_units(h) for h in range(EARLY) for _ in range(3)]
     unit = lambda k: pltpu.VMEM((k, 16, LANES), BF16)
     return pl.pallas_call(
         middle_kernel,
-        in_specs=[vmem()] * 5,
+        in_specs=[vmem()] * 6,
         out_specs=[vmem()] * 6,
         out_shape=[
             shape((seqs, own, d), F32), shape((own, d), BF16), shape((seqs, own, d), BF16),
-            shape((seqs, own, d), BF16), shape((24 * chunk_units(EARLY), 16, LANES), BF16),
+            shape((seqs, own, d), BF16), shape((late_at(len(SPLITS)), 16, LANES), BF16),
             shape((own_at(EARLY, 0), 16, LANES), BF16),
         ],
         scratch_shapes=[pltpu.VMEM(flat, BF16)] * 3
@@ -953,7 +981,7 @@
         + [pltpu.VMEM((seqs, 2, own, d), BF16)] * 2
         + [pltpu.VMEM((own, d), BF16)]
         + [pltpu.VMEM((seqs, 2, own, d), BF16)] * 2
-        + [pltpu.VMEM((own, d), BF16)]
+        + [pltpu.VMEM((own, d), BF16), pltpu.VMEM((size, own, d), BF16)]
         + [unit(24 * chunk_units(h)) for h in range(EARLY)]
         + [unit(4 * k) for k in u]
         + [unit(7 * k) for k in u]
@@ -962,35 +990,38 @@
             pltpu.SemaphoreType.DMA((3 * EARLY, 3)),
             pltpu.SemaphoreType.DMA((3, seqs)),
             pltpu.SemaphoreType.DMA((3, seqs)),
+            pltpu.SemaphoreType.DMA((4, 3)),
+            pltpu.SemaphoreType.DMA((4, 3)),
         ],
         compiler_params=fused(1),
         cost_estimate=cost(27e9, 30e6),
         name="middle",
-    )(n, c, wg, wu, wd)
+    )(n, nb, c, wg, wu, wd)
 
 
 FFN_UNITS = 3 * sum(r for _, r in SPLITS) // 16
 SECOND = 3
 AFTER_EVENTS = {
-    0: (("F00", 3), ("F01", 3), ("F20", 0),),
+    0: (("F00", 3), ("F01", 3), ("F10", 0),),
     1: (("F02", 3),),
-    2: (("F10", 3), ("F22", 0), ("F11", 3), ("F02", 4), ("F12", 3),),
-    4: (("F21", 0), ("O0", 0), ("F11", 4), ("F00", 4), ("O1", 0),),
-    5: (("cross", 0), ("F01", 4),),
-    6: (("F20", 1), ("F21", 1),),
-    7: (("F10", 4), ("O1", 1), ("F22", 1), ("O0", 1),),
-    8: (("F20", 2), ("F02", 5), ("F00", 5), ("F21", 2),),
-    9: (("cross", 1), ("key", 0), ("F12", 4), ("F22", 2),),
-    10: (("F01", 5), ("F20", 3), ("emit", 0),),
-    11: (("O0", 2), ("F11", 5), ("F21", 3), ("F10", 5),),
-    12: (("F22", 3),),
-    13: (("O1", 2), ("F12", 5),),
-    14: (("F21", 4),),
-    15: (("O1", 3), ("F20", 4), ("emit", 1),),
-    "T0": (("O0", 3),),
-    "T1": (("F22", 4), ("O1", 4), ("K0", 0), ("K1", 0), ("O0", 4), ("F20", 5), ("O1", 5), ("F21", 5),),
-    "T2": (("O0", 5), ("K0", 1), ("K2", 0), ("F22", 5), ("K3", 0), ("K1", 1), ("O1", 6),),
-    "T3": (("K4", 0), ("O0", 6), ("K0", 2), ("K2", 1), ("K3", 1), ("O1", 7), ("K1", 2), ("K2", 2), ("K4", 1), ("O0", 7), ("K0", 3), ("K3", 2), ("K2", 3), ("K1", 3), ("K4", 2), ("K0", 4), ("K3", 3), ("K2", 4), ("O1", 8), ("K1", 4), ("K4", 3), ("K3", 4), ("O0", 8), ("K0", 5), ("K1", 5), ("K4", 4), ("K2", 5), ("O1", 9), ("K3", 5), ("K0", 6), ("K4", 5), ("K2", 6), ("O0", 9), ("K1", 6), ("K4", 6), ("K3", 6), ("K0", 7), ("K2", 7), ("K1", 7), ("K3", 7), ("K4", 7), ("K0", 8), ("K3", 8), ("K2", 8), ("K1", 8), ("K0", 9), ("K3", 9), ("K4", 8), ("K2", 9), ("K1", 9), ("K4", 9),),
+    2: (("F11", 0), ("F12", 0), ("F21", 0), ("F20", 0),),
+    3: (("F00", 4), ("O0", 0), ("F01", 4),),
+    4: (("O1", 0), ("F22", 0), ("F10", 1), ("F02", 4),),
+    5: (("cross", 0), ("F12", 1), ("F11", 1),),
+    6: (("F20", 1), ("F10", 2), ("F21", 1), ("O1", 1), ("F22", 1),),
+    7: (("F12", 2), ("F00", 5), ("F11", 2),),
+    8: (("F02", 5), ("F20", 2), ("O0", 1),),
+    9: (("cross", 1), ("key", 0), ("F10", 3), ("F01", 5), ("F21", 2), ("emit", 0),),
+    10: (("O0", 2), ("O1", 2), ("F22", 2),),
+    11: (("F12", 3), ("O1", 3),),
+    12: (("F11", 3),),
+    13: (("F20", 3), ("F10", 4), ("emit", 1),),
+    14: (("F21", 3), ("O0", 3), ("F11", 4), ("F22", 3),),
+    15: (("O1", 4), ("F12", 4), ("F10", 5), ("O0", 4), ("F20", 4),),
+    "T0": (("F21", 4),),
+    "T1": (("O1", 5), ("K0", 0), ("O0", 5), ("K1", 0), ("F11", 5), ("F12", 5), ("F22", 4),),
+    "T2": (("K0", 1), ("K2", 0), ("F20", 5), ("K3", 0), ("O1", 6),),
+    "T3": (("K4", 0), ("F21", 5), ("O0", 6), ("K2", 1), ("K1", 1), ("F22", 5), ("K0", 2), ("O0", 7), ("O1", 7), ("K3", 1), ("K2", 2), ("K4", 1), ("K0", 3), ("K1", 2), ("K3", 2), ("K2", 3), ("K4", 2), ("K0", 4), ("O1", 8), ("K1", 3), ("O0", 8), ("K4", 3), ("K3", 3), ("K2", 4), ("K0", 5), ("K1", 4), ("K4", 4), ("K3", 4), ("O1", 9), ("K2", 5), ("K0", 6), ("K4", 5), ("K1", 5), ("K3", 5), ("O0", 9), ("K2", 6), ("K4", 6), ("K0", 7), ("K1", 6), ("K2", 7), ("K3", 6), ("K4", 7), ("K1", 7), ("K3", 7), ("K0", 8), ("K2", 8), ("K4", 8), ("K0", 9), ("K3", 8), ("K2", 9), ("K4", 9), ("K1", 8), ("K3", 9), ("K1", 9),),
 }
 OUT_PARTS = ("cyxnf", "cxnyf")
 Q_PARTS = ("cxynf", "cnyfx")
@@ -1015,8 +1046,9 @@
     (bq_ref, bk_ref, bv_ref, cap_ref, da_ref, aq_ref, ak_ref, av_ref, tq_ref, tk_ref, tv_ref,
      dm_ref, late_ref, gq_ref, gkp_ref, gkc_ref, gkx_ref, ox_ref, kb_ref, vb_ref, dx_ref, gain_ref) = refs[:22]
     refs = refs[22:]
-    gots, refs = refs[:3], refs[3:]
-    accs, refs = refs[:3], refs[3:]
+    n_late = 3 * (len(SPLITS) - EARLY)
+    gots, refs = refs[:n_late], refs[n_late:]
+    accs, refs = refs[:n_late], refs[n_late:]
     ob, refs = refs[:n_out], refs[n_out:]
     og, refs = refs[:n_out], refs[n_out:]
     oa, refs = refs[:n_out], refs[n_out:]
@@ -1034,12 +1066,13 @@
         for m in range(3):
             i = 3 * h + m
             u = chunk_units(h)
-            late = h == EARLY
+            late = h >= EARLY
+            j = i - 3 * EARLY
             sums[h, m] = Sum(
-                FFN_NAMES[h][m], u, gw_ref if late else None, 8 * u * m,
-                accs[m] if late else None, gots[m] if late else None,
+                FFN_NAMES[h][m], u, gw_ref if late else None, late_at(h) + 8 * u * m,
+                accs[j] if late else None, gots[j] if late else None,
                 gr_ref, m * (half // 3) + off // 16, send.at[i], recv.at[i],
-                local=loc.at[m] if late else None, top=half,
+                local=loc.at[j] if late else None, top=half,
             )
     k0 = len(sums)
     outs = [
@@ -1076,7 +1109,7 @@
         copy.start()
     enter("cxynf")
     for h, m in sums:
-        if h == EARLY:
+        if h >= EARLY:
             sums[h, m].begin()
         else:
             sums[h, m].resume(own_ref, own_at(h, m))
@@ -1329,8 +1362,10 @@
             pltpu.VMEM((own, d), BF16),
             pltpu.VMEM((1, d), F32),
         ]
-        + [pltpu.VMEM((7 * chunk_units(EARLY), 16, LANES), BF16)] * 3
-        + [pltpu.VMEM((4 * chunk_units(EARLY), 16, LANES), BF16)] * 3
+        + [
+            pltpu.VMEM((n * chunk_units(h), 16, LANES), BF16)
+            for n in (7, 4) for h in range(EARLY, len(SPLITS)) for _ in range(3)
+        ]
         + [pltpu.VMEM((n, 16, 1024), BF16) for n in (32, 31, 16) for _ in OUT_PARTS]
         + [
             pltpu.VMEM((n, 16, lanes), BF16) for n in (32, 31, 16)
@@ -1339,7 +1374,7 @@
         + [
             pltpu.SemaphoreType.DMA((total, 10)),
             pltpu.SemaphoreType.DMA((total, 10)),
-            pltpu.SemaphoreType.DMA((3,)),
+            pltpu.SemaphoreType.DMA((3 * (len(SPLITS) - EARLY),)),
             pltpu.SemaphoreType.DMA((5, 2)),
             pltpu.SemaphoreType.DMA((5, 2)),
             pltpu.SemaphoreType.DMA((2, 2)),
@@ -1436,10 +1471,10 @@
     dq = lax.dynamic_slice_in_dim(doc_ids, me * own, own, 1)[:, None, :]
     dk = lax.dynamic_slice_in_dim(doc_ids, first * own, nblk * own, 1)[:, :, None]
     wt = factor_weight.T
-    n1, qf, kvw, att, q, k, v, lse, hm, ng, cg = fore(
+    n1, qf, kvw, att, q, k, v, lse, hm, ng, nb, cg = fore(
         nblk, tokens, wt, output_weight, g1, g2, dq, dk, cotangent
     )
-    dn, ds, ok, os, gw, own_sums = middle(ng, cg, gate_weight.T, up_weight.T, down_weight)
+    dn, ds, ok, os, gw, own_sums = middle(ng, nb, cg, gate_weight.T, up_weight.T, down_weight)
     output, input_grad, gr, go, gf = after(
         nblk, gw, own_sums, dn, ds, ok, os, q, k, v, lse, dq, dk, qf, kvw, hm, cotangent, output_weight,
         g1, g2, att, n1, tokens, wt,

time: 264 us -> 260 us (0.985)
  Pallas kernels: 259 us -> 256 us
    pallas_call x1, Pallas kernels: 119 us -> 131 us  [after(): pl.pallas_call(functools.partial(after_kernel, nblk), in_specs=[hbm() if...]
    pallas_call x1, Pallas kernels: 70.4 us -> 58.9 us  [fore(): pl.pallas_call(functools.partial(fore_kernel, nblk), in_specs=[vmem()] *...]
    pallas_call x1, Pallas kernels: 58.9 us -> 55 us  [middle(): pl.pallas_call(middle_kernel, in_specs=[vmem()] * 6, out_specs=[vmem()] *...]
where the time goes in v1:
time: 260 us
  Pallas kernels  256 us (98%)
  local copies, waits for them, and re-layouts  3.88 us (1%)
    pallas_call x1, Pallas kernels, after(): pl.pallas_call(functools.partial(after_kernel, nblk), in_specs=[hbm() if...  131 us
    pallas_call x1, Pallas kernels, fore(): pl.pallas_call(functools.partial(fore_kernel, nblk), in_specs=[vmem()] *...  58.9 us
    pallas_call x1, Pallas kernels, middle(): pl.pallas_call(middle_kernel, in_specs=[vmem()] * 6, out_specs=[vmem()] *...  55 us
    pallas_call x1, Pallas kernels, finish_all(): pl.pallas_call(last_kernel, grid=(steps,), in_specs=[tokens, tokens, pl.B...  10.7 us

profile of v1, /device:TPU:0, one launch (start us, length us, event | category | flops | bytes accessed | tf_op | source)
XLA Modules:
  0.0 260.1 jit_solution(9878349005919828043)
XLA Ops:
  0.6 0.0 copy-start
  0.7 0.7 copy-done
  1.3 0.6 broadcast_in_dim.14.dq_ref
  1.9 1.2 copy.19.dk_ref
  3.1 58.9 %fore.1 = (bf16[2,256,1024]{2,1,0:T(8,128)(2,1)}, bf16[2,256,512]{2,1,0:T(8,128)(2,1)}, bf16[2,768,384]{2,1,0:T(8,128)(2,1)}, bf16[2,256,1024]{2,1,0:T(8,128)(2,...) custom-call(bf16[2,256,1024]{2,1,0:T(8,128)(2,1)} %x_ref.3, ...), custom_call_target="tpu_custom_call" | custom-call | flops 30000001024 | bytes 30000000 | tf_op jit(solution)/shard_map/fore/pallas_call | solution.py:766
  62.1 55.0 %middle.1 = (f32[2,256,1024]{2,1,0:T(8,128)}, bf16[256,1024]{1,0:T(8,128)(2,1)}, bf16[2,256,1024]{2,1,0:T(8,128)(2,1)}, bf16[2,256,1024]{2,1,0:T(8,128)(2,1)}, b...) custom-call(bf16[4,256,1024]{2,1,0:T(8,128)(2,1)} %get-tuple-element.45.n_ref, ...), custom_call_target="tpu_custom_call" | custom-call | flops 27000000512 | bytes 30000000 | tf_op jit(solution)/shard_map/middle/pallas_call | solution.py:970
  117.1 130.9 %after.1 = (bf16[2,256,1024]{2,1,0:T(8,128)(2,1)}, bf16[2,256,1024]{2,1,0:T(8,128)(2,1)}, bf16[264,16,512]{2,1,0:T(8,128)(2,1)}, bf16[32,16,1024]{2,1,0:T(8,128)...) custom-call(bf16[192,16,512]{2,1,0:T(8,128)(2,1)} %get-tuple-element, ...), custom_call_target="tpu_custom_call" | custom-call | flops 60000002048 | bytes 60000000 | tf_op jit(solution)/shard_map/after/pallas_call | solution.py:1333
  247.9 0.0 copy-start.1
  247.9 10.7 %last.1 = (bf16[2,256,1024]{2,1,0:T(8,128)(2,1)}, bf16[2,256,1024]{2,1,0:T(8,128)(2,1)}, f32[704,1024]{1,0:T(8,128)}, f32[704,1024]{1,0:T(8,128)}, f32[704,1024]...) custom-call(bf16[2,256,1024]{2,1,0:T(8,128)(2,1)} %get-tuple-element.63.out_ref, ...), custom_call_target="tpu_custom_call" | custom-call | flops 1000000 | bytes 30000000 | tf_op jit(solution)/shard_map/last/pallas_call | solution.py:1446
  258.7 1.4 fusion
  260.1 0.0 copy-done.1
  (2 shorter events, 0.0 us)
Async XLA Ops:
  0.6 0.7 copy-start
  247.9 12.2 %copy-start.1 = (s32[2,1024]{1,0:T(2,128)S(1)}, s32[2,1024]{1,0:T(2,128)}, u32[]{:S(2)}) copy-start(s32[2,1024]{1,0:T(2,128)} %param.11) | copy-start | bytes 24580

commit v2 on v1

--- a/solution.py
+++ b/solution.py
@@ -647,7 +647,10 @@
     first = me // 3
     kvs = [Gather(kvg_ref.at[s], send.at[s], recv.at[s]) for s in range(seqs)]
     cots = [Gather(cg_ref.at[s], send.at[2 + s], recv.at[2 + s]) for s in range(seqs)]
-    norm = Gather(ng_ref, send.at[4], recv.at[4])
+    norms = [
+        Gather(ng_ref, send.at[4 + i], recv.at[4 + i], pl.ds(i * (own // 4), own // 4))
+        for i in range(4)
+    ]
     for s in range(seqs):
         cg_ref[s, 0] = c_ref[s]
     for s in range(seqs):
@@ -719,7 +722,8 @@
             @pl.when(s == 0)
             def _():
                 ng_ref[0] = n2
-                norm.first()
+                for norm in norms:
+                    norm.first()
 
             @pl.when(s == 1)
             def _():
@@ -740,8 +744,9 @@
         return carry
 
     lax.fori_loop(0, seqs * PAIRS, step, 0)
-    norm.relay()
-    for each in cots + [norm]:
+    for norm in norms:
+        norm.relay()
+    for each in cots + norms:
         each.done()
 
 
@@ -782,8 +787,8 @@
             pltpu.VMEM((win, RK * 128), F32),
             pltpu.VMEM((win, own), F32),
             pltpu.VMEM((PAIRS, own, 128), BF16),
-            pltpu.SemaphoreType.DMA((5, 3)),
-            pltpu.SemaphoreType.DMA((5, 3)),
+            pltpu.SemaphoreType.DMA((8, 3)),
+            pltpu.SemaphoreType.DMA((8, 3)),
         ],
         compiler_params=fused(0),
         cost_estimate=cost(30e9, 30e6),
@@ -1403,8 +1408,7 @@
 
         @pl.when(step // 2 == g)
         def _(ref=ref):
-            half = pl.ds((step % 2) * 16, 16)
-            go_ref[...] = ref[half].reshape(256, 1024).astype(F32)
+            go_ref[...] = ref[...].reshape(256, 1024).astype(F32)
 
     rows = pl.ds(pl.multiple_of(step * 128, 128), 128)
     for i, ref in enumerate((q0_ref, q1_ref)):
@@ -1449,7 +1453,9 @@
         in_specs=[
             tokens, tokens,
             pl.BlockSpec((2, 3, ff // 16 // steps, 16, LANES), lambda i: (0, 0, i, 0, 0)),
-        ] + [whole(a) for a in list(go) + list(gf)],
+            pl.BlockSpec((16, 16, d), lambda i: (jnp.minimum(i, 1), 0, 0)),
+            pl.BlockSpec((16, 16, d), lambda i: (jnp.maximum(i - 2, 0), 0, 0)),
+        ] + [whole(a) for a in gf],
         out_specs=[tokens, tokens, rows(ff), rows(ff), rows(ff), rows(d), whole(outs[6]), whole(outs[7])],
         out_shape=outs,
         compiler_params=params(),

time: 260 us -> 260 us (level)
  no operation moved by 1% of the time
where the time goes in v2:
time: 260 us
  Pallas kernels  255 us (98%)
  local copies, waits for them, and re-layouts  3.88 us (1%)
    pallas_call x1, Pallas kernels, after(): pl.pallas_call(functools.partial(after_kernel, nblk), in_specs=[hbm() if...  131 us
    pallas_call x1, Pallas kernels, fore(): pl.pallas_call(functools.partial(fore_kernel, nblk), in_specs=[vmem()] *...  58.6 us
    pallas_call x1, Pallas kernels, middle(): pl.pallas_call(middle_kernel, in_specs=[vmem()] * 6, out_specs=[vmem()] *...  54.9 us
    pallas_call x1, Pallas kernels, finish_all(): pl.pallas_call(last_kernel, grid=(steps,), in_specs=[tokens, tokens, pl.B...  11 us

profile of v2, /device:TPU:0, one launch (start us, length us, event | category | flops | bytes accessed | tf_op | source)
XLA Modules:
  0.0 259.8 jit_solution(14157265933928945545)
XLA Ops:
  0.6 0.0 copy-start
  0.7 0.7 copy-done
  1.3 0.6 broadcast_in_dim.14.dq_ref
  1.9 1.2 copy.19.dk_ref
  3.1 58.6 %fore.1 = (bf16[2,256,1024]{2,1,0:T(8,128)(2,1)}, bf16[2,256,512]{2,1,0:T(8,128)(2,1)}, bf16[2,768,384]{2,1,0:T(8,128)(2,1)}, bf16[2,256,1024]{2,1,0:T(8,128)(2,...) custom-call(bf16[2,256,1024]{2,1,0:T(8,128)(2,1)} %x_ref.3, ...), custom_call_target="tpu_custom_call" | custom-call | flops 30000001024 | bytes 30000000 | tf_op jit(solution)/shard_map/fore/pallas_call | solution.py:771
  61.7 54.9 %middle.1 = (f32[2,256,1024]{2,1,0:T(8,128)}, bf16[256,1024]{1,0:T(8,128)(2,1)}, bf16[2,256,1024]{2,1,0:T(8,128)(2,1)}, bf16[2,256,1024]{2,1,0:T(8,128)(2,1)}, b...) custom-call(bf16[4,256,1024]{2,1,0:T(8,128)(2,1)} %get-tuple-element.45.n_ref, ...), custom_call_target="tpu_custom_call" | custom-call | flops 27000000512 | bytes 30000000 | tf_op jit(solution)/shard_map/middle/pallas_call | solution.py:975
  116.6 130.8 %after.1 = (bf16[2,256,1024]{2,1,0:T(8,128)(2,1)}, bf16[2,256,1024]{2,1,0:T(8,128)(2,1)}, bf16[264,16,512]{2,1,0:T(8,128)(2,1)}, bf16[32,16,1024]{2,1,0:T(8,128)...) custom-call(bf16[192,16,512]{2,1,0:T(8,128)(2,1)} %get-tuple-element, ...), custom_call_target="tpu_custom_call" | custom-call | flops 60000002048 | bytes 60000000 | tf_op jit(solution)/shard_map/after/pallas_call | solution.py:1338
  247.4 0.0 copy-start.1
  247.4 11.0 %last.1 = (bf16[2,256,1024]{2,1,0:T(8,128)(2,1)}, bf16[2,256,1024]{2,1,0:T(8,128)(2,1)}, f32[704,1024]{1,0:T(8,128)}, f32[704,1024]{1,0:T(8,128)}, f32[704,1024]...) custom-call(bf16[2,256,1024]{2,1,0:T(8,128)(2,1)} %get-tuple-element.63.out_ref, ...), custom_call_target="tpu_custom_call" | custom-call | flops 1000000 | bytes 30000000 | tf_op jit(solution)/shard_map/last/pallas_call | solution.py:1450
  258.4 1.4 fusion
  259.8 0.0 copy-done.1
  (2 shorter events, 0.0 us)
Async XLA Ops:
  0.6 0.7 copy-start
  247.4 12.4 %copy-start.1 = (s32[2,1024]{1,0:T(2,128)S(1)}, s32[2,1024]{1,0:T(2,128)}, u32[]{:S(2)}) copy-start(s32[2,1024]{1,0:T(2,128)} %param.11) | copy-start | bytes 24580
